TPU v7x, 1024 devices: a whole 4x8x16 slice. The times are simulated.
1024 devices in a mesh: blk: 128 (over y, z), sub: 8 (over x, core).
Axes of the slice: x: 4, y: 8, z: 16, core: 2. Of those that a mesh axis runs over, the one named last changes fastest.
Arguments:
- east_flow: float32 [2048, 12, 7168], P(('blk', 'sub')), may hold values from -6 to 6
- north_flow: float32 [2048, 12, 7168], P(('blk', 'sub')), may hold values from -6 to 6
- levels: int32 [2048, 7168], P(('blk', 'sub')), may hold values from 0 to 12
- coriolis: float32 [2048], P(('blk', 'sub')), may hold values from -1 to 1
- thickness: float32 [12], replicated, may hold values from 0.02 to 0.12
- surface: float32 [2048, 7168], P('blk', 'sub'), may hold values from -6 to 6
Outputs:
- east_next: float32 [2048, 12, 7168], P(('blk', 'sub'))
- north_next: float32 [2048, 12, 7168], P(('blk', 'sub'))
- surface_next: float32 [2048, 7168], P('blk', 'sub')
Inputs may be any that keep to these rules, and one draw needn't show every extreme that they name: levels[j,i] active levels of the column counted from the top, 0 on land, up to 12.
All inputs are finite; a program needn't handle non-finite values.
Results may differ from a plain program's by a relative error of at most 0.00002.
Values sent between devices are 32-bit elements; how exact they have to be, the bound alone decides.
A program may use at most 64 MiB of HBM per device.

v0:
```python
import jax
import jax.numpy as jnp
from jax import lax
from jax.sharding import Mesh
from jax.sharding import PartitionSpec as P

NSUB = 4
BLK_SUB = ("blk", "sub_0", "sub_1")
SUB = ("sub_0", "sub_1")


second_weights = (-1.0 / 12.0, 16.0 / 12.0, -30.0 / 12.0, 16.0 / 12.0, -1.0 / 12.0)
first_weights = (1.0 / 12.0, -8.0 / 12.0, 0.0, 8.0 / 12.0, -1.0 / 12.0)
viscosity = 0.05
mixing = 0.1
rotation = 0.2
continuity = 0.5
pressure = 0.5


def with_halo(array, sides, width):
    edges = {}
    for axis, dim in sides:
        devices, length = (lax.axis_size(axis), array.shape[dim])
        up = [(i, (i + 1) % devices) for i in range(devices - 1)]
        last = lax.slice_in_dim(array, length - width, length, axis=dim)
        leading = lax.slice_in_dim(array, 0, width, axis=dim)
        edges[dim] = (
            lax.ppermute(last, axis, up),
            lax.ppermute(leading, axis, [(b, a) for a, b in up]),
        )
    done = []
    for _, dim in sides:
        low, high = edges[dim]
        around = [(width, width) if d in done else (0, 0) for d in range(array.ndim)]
        array = jnp.concatenate([jnp.pad(low, around), array, jnp.pad(high, around)], axis=dim)
        done.append(dim)
    return array


def split_up(array, dim, devices):
    before, after = (array.shape[:dim], array.shape[dim + 1 :])
    return jnp.moveaxis(array.reshape(*before, devices, -1, *after), dim, 0)


def joined_along(pieces, dim):
    dims = list(pieces.shape[1:])
    dims[dim] *= pieces.shape[0]
    return jnp.moveaxis(pieces, 0, dim).reshape(dims)


def moved_by_axis(pieces, axes, order):
    inside = pieces.shape[1:]
    out = pieces.reshape(*(lax.axis_size(a) for a in axes), *inside)
    for k in order:
        out = lax.all_to_all(out, axes[k], k, k, tiled=True)
    return out.reshape(-1, *inside)


def stepwise_exchange(array, axes, order, split_dim, concat_dim):
    pieces = split_up(array, split_dim, lax.axis_size(axes))
    return joined_along(moved_by_axis(pieces, axes, order), concat_dim)


def extended(array, sides, width):
    for axis, dim in sides:
        devices, length = (lax.axis_size(axis), array.shape[dim])
        up = [(i, (i + 1) % devices) for i in range(devices)]
        down = [(j, i) for i, j in up]
        last = lax.slice_in_dim(array, length - width, length, axis=dim)
        leading = lax.slice_in_dim(array, 0, width, axis=dim)
        before = lax.ppermute(last, axis, up)
        after = lax.ppermute(leading, axis, down)
        array = jnp.concatenate([before, array, after], axis=dim)
    return array


def stencil(padded, along, weights):
    length = padded.shape[along] - 4
    total = None
    for offset in range(5):
        if weights[offset] != 0.0:
            term = weights[offset] * lax.slice_in_dim(padded, offset, offset + length, axis=along)
            total = term if total is None else total + term
    return total


def periodic(field, weights):
    total = None
    for offset in range(5):
        term = weights[offset] * jnp.roll(field, 2 - offset, axis=-1)
        total = term if total is None else total + term
    return total


def vertical(field, along):
    count = field.shape[along]
    upper = lax.slice_in_dim(field, 0, 1, axis=along)
    lower = lax.slice_in_dim(field, count - 1, count, axis=along)
    padded = jnp.concatenate((upper, field, lower), axis=along)
    return (
        lax.slice_in_dim(padded, 2, count + 2, axis=along)
        - 2.0 * field
        + lax.slice_in_dim(padded, 0, count, axis=along)
    )


def grid_edges(padded, width):
    count = padded.shape[-2]
    row_ids = lax.broadcasted_iota(jnp.int32, (count, 1), 0)
    place = lax.axis_index("blk")
    final = lax.axis_size("blk") - 1
    below = jnp.logical_and(row_ids < width, place == 0)
    above = jnp.logical_and(row_ids >= count - width, place == final)
    keep = jnp.logical_not(jnp.logical_or(below, above))
    return jnp.where(keep, padded, 0.0)


def body(east_flow, north_flow, levels, coriolis, thickness, surface):
    depth_ids = lax.broadcasted_iota(jnp.int32, east_flow.shape, 1)
    wet = (depth_ids < levels[:, None, :]).astype(jnp.float32)
    east = east_flow * wet
    north = north_flow * wet
    paired = jnp.stack((east, north))
    others = jnp.stack((north, east))
    factors = jnp.array([1.0, -1.0], jnp.float32)[:, None, None, None]
    rotor = coriolis[None, :, None, None]
    padded = with_halo(paired, ((BLK_SUB, 1),), 2)
    laplace = stencil(padded, 1, second_weights) + periodic(paired, second_weights)
    starred = wet[None] * (
        paired
        + viscosity * laplace
        + mixing * vertical(paired, 2)
        + factors * rotation * rotor * others
    )
    layer = thickness[None, None, :, None]
    sums = jnp.sum(layer * starred, axis=2)
    depth = jnp.sum(thickness[None, :, None] * wet, axis=1)
    forcing = jnp.concatenate((sums, depth[None]), axis=0)
    blocked = stepwise_exchange(forcing, SUB, (1, 0), 2, 1)
    east_tr = blocked[0]
    north_tr = blocked[1]
    block_depth = blocked[2]
    height = surface
    for substep in range(NSUB):
        rims = grid_edges(
            extended(jnp.stack((height, east_tr, north_tr)), (("blk", 1), (SUB, 2)), 4), 4
        )
        widened = rims[0, 2:-2, 2:-2] - continuity * (
            stencil(rims[1, 2:-2, :], 1, first_weights)
            + stencil(rims[2, :, 2:-2], 0, first_weights)
        )
        widened = grid_edges(widened, 2)
        east_tr = east_tr - pressure * block_depth * stencil(widened[2:-2, :], 1, first_weights)
        north_tr = north_tr - pressure * block_depth * stencil(widened[:, 2:-2], 0, first_weights)
        height = widened[2:-2, 2:-2]
    changes = jnp.stack((east_tr, north_tr)) - blocked[:2]
    banded = lax.all_to_all(changes, SUB, split_axis=1, concat_axis=2, tiled=True)
    inverse = jnp.where(levels > 0, 1.0 / jnp.where(levels > 0, depth, 1.0), 0.0)
    east_next = starred[0] + wet * (banded[0] * inverse)[:, None, :]
    north_next = starred[1] + wet * (banded[1] * inverse)[:, None, :]
    return (east_next, north_next, height)


def solution(mesh):
    split = Mesh(mesh.devices.reshape(mesh.shape["blk"], 4, 2), ("blk", "sub_0", "sub_1"))
    placed = (
        P(BLK_SUB, None, None),
        P(BLK_SUB, None, None),
        P(BLK_SUB, None),
        P(BLK_SUB),
        P(),
        P("blk", SUB),
    )
    return jax.shard_map(
        body,
        mesh=split,
        in_specs=placed,
        out_specs=(P(BLK_SUB, None, None), P(BLK_SUB, None, None), P("blk", SUB)),
        check_vma=False,
    )
```

profile of v0, /device:TPU:1, one launch (start us, length us, event | category | flops | bytes accessed | tf_op | source)
XLA Modules:
  0.0 150.4 jit_solution(1896487657320209796)
XLA Ops:
  0.6 2.2 %select_reduce_fusion = (f32[2,7168]{1,0:T(2,128)S(1)}, f32[1,2,12,7168]{3,1,2,0:T(2,128)S(1)}, f32[1,2,12,7168]{3,1,2,0:T(2,128)S(1)}) fusion(f32[12]{0:T(128)} %param.11, s32[2,7168]{1,0:T(2,128)} %param.9, f32[2,12,7168]{2,0,1:T(2,128)} %param.8, f32[2,12,7168]{2,0,1:T(2,128)} %param.7), kind=kLoop, calls=%fused_computation.60 | loop fusion | flops 845824 | bytes 2867248 | tf_op jit(solution)/shard_map/reduce_sum | solution.py:138
  3.5 4.5 %collective-permute-start = (f32[2,2,12,7168]{3,1,2,0:T(2,128)S(1)}, f32[2,2,12,7168]{3,1,2,0:T(2,128)S(1)}, u32[]{:S(2)}, u32[]{:S(2)}) collective-permute-start(f32[2,2,12,7168]{3,1,2,0:T(2,128)S(1)} %pad_maximum_fusion), channel_id=1, source_target_pairs={{0,1},{1,2},{2,3},{3,4},{4,5},{5,6},{6,7},{7,8},{8,9},{9,10},{10,1... | collective-permute-start | bytes 4128776 | tf_op jit(solution)/shard_map/ppermute | solution.py:29
  8.0 12.9 %collective-permute-start.1 = (f32[2,2,12,7168]{3,1,2,0:T(2,128)S(1)}, f32[2,2,12,7168]{3,1,2,0:T(2,128)S(1)}, u32[]{:S(2)}, u32[]{:S(2)}) collective-permute-start(f32[2,2,12,7168]{3,1,2,0:T(2,128)S(1)} %pad_maximum_fusion), channel_id=1, source_target_pairs={{1,0},{2,1},{3,2},{4,3},{5,4},{6,5},{7,6},{8,7},{9,8},{10,9},{11,1... | collective-permute-start | bytes 4128776 | tf_op jit(solution)/shard_map/ppermute | solution.py:30
  20.9 2.4 %fusion.1 = (f32[2,2,12,7167]{3,1,2,0:T(2,128)S(1)}, f32[2,2,12,7167]{3,1,2,0:T(2,128)S(1)}) fusion(f32[1,2,12,7168]{3,1,2,0:T(2,128)S(1)} %get-tuple-element.54, f32[1,2,12,7168]{3,1,2,0:T(2,128)S(1)} %get-tuple-element.53), kind=kLoop, calls=%fused_computation.22 | loop fusion | flops 688032 | bytes 4128384 | tf_op jit(solution)/shard_map/stack | solution.py:124
  23.3 2.4 %fusion = (f32[2,2,12,7166]{3,1,2,0:T(2,128)S(1)}, f32[2,2,12,7166]{3,1,2,0:T(2,128)S(1)}) fusion(f32[1,2,12,7168]{3,1,2,0:T(2,128)S(1)} %get-tuple-element.54, f32[1,2,12,7168]{3,1,2,0:T(2,128)S(1)} %get-tuple-element.53), kind=kLoop, calls=%fused_computation.21 | loop fusion | flops 687936 | bytes 4128000 | tf_op jit(solution)/shard_map/stack | solution.py:124
  27.6 15.3 %multiply_reduce_fusion = (f32[2,2,7168]{2,1,0:T(2,128)S(1)}, f32[2,2,12,7168]{3,1,2,0:T(2,128)S(1)}) fusion(f32[12]{0:T(128)S(1)} %copy-done.2, f32[1,2,12,7168]{3,1,2,0:T(2,128)S(1)} %get-tuple-element.54, f32[1,2,12,7168]{3,1,2,0:T(2,128)S(1)} %get-tuple-element.53, f32[2,2]{1,0:T(2,128)S(1)} %broadcast_multiply_fusion, ...), kind=kLoop, calls=%fused_computation.54 | loop fusion | flops 15110144 | bytes 12042304 | tf_op jit(solution)/shard_map/reduce_sum | solution.py:137
  43.1 3.5 %all_to_all.25 = f32[4,2,3,2,896]{4,3,0,2,1:T(2,128)S(1)} all-to-all(f32[4,2,3,2,896]{4,3,0,2,1:T(2,128)S(1)} %copy.25), channel_id=1, replica_groups=mesh['blk'=128,'sub_0'=4,'sub_1'=2] {'sub_1'}, dimensions={1} | all-to-all | bytes 344064 | tf_op jit(solution)/shard_map/all_to_all | solution.py:56
  47.3 6.7 %all-to-all-start.1 = ((f32[4,2,3,2,896]{4,3,1,2,0:T(2,128)}), f32[4,2,3,2,896]{4,3,1,2,0:T(2,128)S(1)}, u32[]{:S(2)}, u32[]{:S(2)}) async-start(f32[4,2,3,2,896]{4,3,1,2,0:T(2,128)} %copy.26), calls=%async_computation.1 | async-start | bytes 344064 | tf_op jit(solution)/shard_map/all_to_all | solution.py:56
  54.0 5.1 %all-to-all-done.1 = f32[4,2,3,2,896]{4,3,1,2,0:T(2,128)S(1)} async-done(((f32[4,2,3,2,896]{4,3,1,2,0:T(2,128)}), f32[4,2,3,2,896]{4,3,1,2,0:T(2,128)S(1)}, u32[]{:S(2)}, u32[]{:S(2)}) %all-to-all-start.1) | async-done | bytes 172064 | tf_op jit(solution)/shard_map/all_to_all | solution.py:56
  59.3 4.0 %collective-permute-start.2 = (f32[3,4,896]{2,1,0:T(4,128)S(1)}, f32[3,4,896]{2,1,0:T(4,128)S(1)}, u32[]{:S(2)}, u32[]{:S(2)}) collective-permute-start(f32[3,4,896]{2,1,0:T(4,128)S(1)} %get-tuple-element.33), channel_id=1, source_target_pairs={{0,8},{8,16},{16,24},{24,32},{32,40},{40,48},{48,56},{56,64},{64,7... | collective-permute-start | bytes 129032 | tf_op jit(solution)/shard_map/ppermute | solution.py:72
  63.3 16.4 %collective-permute-start.3 = (f32[3,4,896]{2,1,0:T(4,128)S(1)}, f32[3,4,896]{2,1,0:T(4,128)S(1)}, u32[]{:S(2)}, u32[]{:S(2)}) collective-permute-start(f32[3,4,896]{2,1,0:T(4,128)S(1)} %get-tuple-element.34), channel_id=1, source_target_pairs={{8,0},{16,8},{24,16},{32,24},{40,32},{48,40},{56,48},{64,56},{72,6... | collective-permute-start | bytes 129032 | tf_op jit(solution)/shard_map/ppermute | solution.py:73
  79.7 1.1 collective-permute-done.3
  80.8 2.5 %collective-permute-start.4 = (f32[3,24,4]{2,1,0:T(8,128)S(1)}, f32[3,24,4]{2,1,0:T(8,128)S(1)}, u32[]{:S(2)}, u32[]{:S(2)}) collective-permute-start(f32[3,24,4]{2,1,0:T(8,128)S(1)} %get-tuple-element.25), channel_id=1, source_target_pairs={{0,1},{1,2},{2,3},{3,4},{4,5},{5,6},{6,7},{7,0},{8,9},{9,10},{10,1... | collective-permute-start | bytes 3464 | tf_op jit(solution)/shard_map/ppermute | solution.py:72
  83.5 0.9 collective-permute-done.4
  84.4 2.6 %collective-permute-done.5 = f32[3,24,4]{2,1,0:T(8,128)S(1)} collective-permute-done((f32[3,24,4]{2,1,0:T(8,128)S(1)}, f32[3,24,4]{2,1,0:T(8,128)S(1)}, u32[]{:S(2)}, u32[]{:S(2)}) %collective-permute-start.5) | collective-permute-done | bytes 1184 | tf_op jit(solution)/shard_map/ppermute | solution.py:73
  87.8 1.9 %collective-permute-start.6 = (f32[3,4,896]{2,1,0:T(4,128)S(1)}, f32[3,4,896]{2,1,0:T(4,128)S(1)}, u32[]{:S(2)}, u32[]{:S(2)}) collective-permute-start(f32[3,4,896]{2,1,0:T(4,128)S(1)} %get-tuple-element.31), channel_id=1, source_target_pairs={{0,8},{8,16},{16,24},{24,32},{32,40},{40,48},{48,56},{56,64},{64,7... | collective-permute-start | bytes 129032 | tf_op jit(solution)/shard_map/ppermute | solution.py:72
  89.7 7.3 %collective-permute-start.7 = (f32[3,4,896]{2,1,0:T(4,128)S(1)}, f32[3,4,896]{2,1,0:T(4,128)S(1)}, u32[]{:S(2)}, u32[]{:S(2)}) collective-permute-start(f32[3,4,896]{2,1,0:T(4,128)S(1)} %get-tuple-element.32), channel_id=1, source_target_pairs={{8,0},{16,8},{24,16},{32,24},{40,32},{48,40},{56,48},{64,56},{72,6... | collective-permute-start | bytes 129032 | tf_op jit(solution)/shard_map/ppermute | solution.py:73
  97.0 1.1 collective-permute-done.7
  98.8 1.1 collective-permute-start.9
  100.5 1.6 %collective-permute-done.9 = f32[3,24,4]{2,1,0:T(8,128)S(1)} collective-permute-done((f32[3,24,4]{2,1,0:T(8,128)S(1)}, f32[3,24,4]{2,1,0:T(8,128)S(1)}, u32[]{:S(2)}, u32[]{:S(2)}) %collective-permute-start.9) | collective-permute-done | bytes 1184 | tf_op jit(solution)/shard_map/ppermute | solution.py:73
  102.9 1.9 %collective-permute-start.10 = (f32[3,4,896]{2,1,0:T(4,128)S(1)}, f32[3,4,896]{2,1,0:T(4,128)S(1)}, u32[]{:S(2)}, u32[]{:S(2)}) collective-permute-start(f32[3,4,896]{2,1,0:T(4,128)S(1)} %get-tuple-element.29), channel_id=1, source_target_pairs={{0,8},{8,16},{16,24},{24,32},{32,40},{40,48},{48,56},{56,64},{64,7... | collective-permute-start | bytes 129032 | tf_op jit(solution)/shard_map/ppermute | solution.py:72
  104.8 7.3 %collective-permute-start.11 = (f32[3,4,896]{2,1,0:T(4,128)S(1)}, f32[3,4,896]{2,1,0:T(4,128)S(1)}, u32[]{:S(2)}, u32[]{:S(2)}) collective-permute-start(f32[3,4,896]{2,1,0:T(4,128)S(1)} %get-tuple-element.30), channel_id=1, source_target_pairs={{8,0},{16,8},{24,16},{32,24},{40,32},{48,40},{56,48},{64,56},{72,6... | collective-permute-start | bytes 129032 | tf_op jit(solution)/shard_map/ppermute | solution.py:73
  112.1 1.1 collective-permute-done.11
  113.3 0.9 collective-permute-start.12
  114.2 2.3 %collective-permute-start.13 = (f32[3,24,4]{2,1,0:T(8,128)S(1)}, f32[3,24,4]{2,1,0:T(8,128)S(1)}, u32[]{:S(2)}, u32[]{:S(2)}) collective-permute-start(f32[3,24,4]{2,1,0:T(8,128)S(1)} %get-tuple-element.22), channel_id=1, source_target_pairs={{1,0},{2,1},{3,2},{4,3},{5,4},{6,5},{7,6},{0,7},{9,8},{10,9},{11,1... | collective-permute-start | bytes 3464 | tf_op jit(solution)/shard_map/ppermute | solution.py:73
  118.3 1.9 %collective-permute-start.14 = (f32[3,4,896]{2,1,0:T(4,128)S(1)}, f32[3,4,896]{2,1,0:T(4,128)S(1)}, u32[]{:S(2)}, u32[]{:S(2)}) collective-permute-start(f32[3,4,896]{2,1,0:T(4,128)S(1)} %get-tuple-element.27), channel_id=1, source_target_pairs={{0,8},{8,16},{16,24},{24,32},{32,40},{40,48},{48,56},{56,64},{64,7... | collective-permute-start | bytes 129032 | tf_op jit(solution)/shard_map/ppermute | solution.py:72
  120.2 7.3 %collective-permute-start.15 = (f32[3,4,896]{2,1,0:T(4,128)S(1)}, f32[3,4,896]{2,1,0:T(4,128)S(1)}, u32[]{:S(2)}, u32[]{:S(2)}) collective-permute-start(f32[3,4,896]{2,1,0:T(4,128)S(1)} %get-tuple-element.28), channel_id=1, source_target_pairs={{8,0},{16,8},{24,16},{32,24},{40,32},{48,40},{56,48},{64,56},{72,6... | collective-permute-start | bytes 129032 | tf_op jit(solution)/shard_map/ppermute | solution.py:73
  127.5 1.1 collective-permute-done.15
  128.7 0.9 collective-permute-start.16
  129.5 3.5 %collective-permute-start.17 = (f32[3,24,4]{2,1,0:T(8,128)S(1)}, f32[3,24,4]{2,1,0:T(8,128)S(1)}, u32[]{:S(2)}, u32[]{:S(2)}) collective-permute-start(f32[3,24,4]{2,1,0:T(8,128)S(1)} %get-tuple-element.20), channel_id=1, source_target_pairs={{1,0},{2,1},{3,2},{4,3},{5,4},{6,5},{7,6},{0,7},{9,8},{10,9},{11,1... | collective-permute-start | bytes 3464 | tf_op jit(solution)/shard_map/ppermute | solution.py:73
  135.5 12.8 %all_to_all.26 = f32[2,16,896]{2,0,1:T(2,128)S(1)} all-to-all(f32[2,16,896]{2,0,1:T(2,128)S(1)} %maximum_subtract_fusion), channel_id=1, replica_groups=mesh['blk'=128,'sub_0'=4,'sub_1'=2] {'sub_0','sub_1'}, dimensions={1} | all-to-all | bytes 229376 | tf_op jit(solution)/shard_map/all_to_all | solution.py:158
  148.6 1.8 %fusion.21 = (f32[2,12,7168]{2,0,1:T(2,128)}, f32[2,12,7168]{2,0,1:T(2,128)}) fusion(f32[2,2,12,7168]{3,1,2,0:T(2,128)S(1)} %get-tuple-element.6, f32[2,7168]{1,0:T(2,128)S(1)} %get-tuple-element.3, s32[2,7168]{1,0:T(2,128)S(1)} %copy-done, f32[2,7168]{1,0:T(2,128)S(1)} %mul.492), kind=kLoop, calls=%fused_computation.57 | loop fusion | flops 860160 | bytes 2924544 | tf_op jit(solution)/shard_map/add | solution.py:161
  (79 shorter events, 11.0 us)
Async XLA Ops:
  3.5 23.5 %collective-permute-start = (f32[2,2,12,7168]{3,1,2,0:T(2,128)S(1)}, f32[2,2,12,7168]{3,1,2,0:T(2,128)S(1)}, u32[]{:S(2)}, u32[]{:S(2)}) collective-permute-start(f32[2,2,12,7168]{3,1,2,0:T(2,128)S(1)} %pad_maximum_fusion), channel_id=1, source_target_pairs={{0,1},{1,2},{2,3},{3,4},{4,5},{5,6},{6,7},{7,8},{8,9},{9,10},{10,1... | collective-permute-start | bytes 4128776 | tf_op jit(solution)/shard_map/ppermute | solution.py:29
  8.0 19.6 %collective-permute-start.1 = (f32[2,2,12,7168]{3,1,2,0:T(2,128)S(1)}, f32[2,2,12,7168]{3,1,2,0:T(2,128)S(1)}, u32[]{:S(2)}, u32[]{:S(2)}) collective-permute-start(f32[2,2,12,7168]{3,1,2,0:T(2,128)S(1)} %pad_maximum_fusion), channel_id=1, source_target_pairs={{1,0},{2,1},{3,2},{4,3},{5,4},{6,5},{7,6},{8,7},{9,8},{10,9},{11,1... | collective-permute-start | bytes 4128776 | tf_op jit(solution)/shard_map/ppermute | solution.py:30
  25.9 0.7 copy-start.3
  25.9 0.7 copy-start.4
  25.9 0.8 copy-start
  26.0 1.6 %copy-start.2 = (f32[12]{0:T(128)S(1)}, f32[12]{0:T(128)}, u32[]{:S(2)}) copy-start(f32[12]{0:T(128)} %param.11) | copy-start | bytes 148
  43.0 16.2 %copy-start.1 = (f32[16,896]{1,0:T(8,128)S(1)}, f32[16,896]{1,0:T(8,128)}, u32[]{:S(2)}) copy-start(f32[16,896]{1,0:T(8,128)} %param.12) | copy-start | bytes 172036
  47.3 11.7 %all-to-all-start.1 = ((f32[4,2,3,2,896]{4,3,1,2,0:T(2,128)}), f32[4,2,3,2,896]{4,3,1,2,0:T(2,128)S(1)}, u32[]{:S(2)}, u32[]{:S(2)}) async-start(f32[4,2,3,2,896]{4,3,1,2,0:T(2,128)} %copy.26), calls=%async_computation.1 | async-start | bytes 344064 | tf_op jit(solution)/shard_map/all_to_all | solution.py:56
  59.3 20.4 %collective-permute-start.2 = (f32[3,4,896]{2,1,0:T(4,128)S(1)}, f32[3,4,896]{2,1,0:T(4,128)S(1)}, u32[]{:S(2)}, u32[]{:S(2)}) collective-permute-start(f32[3,4,896]{2,1,0:T(4,128)S(1)} %get-tuple-element.33), channel_id=1, source_target_pairs={{0,8},{8,16},{16,24},{24,32},{32,40},{40,48},{48,56},{56,64},{64,7... | collective-permute-start | bytes 129032 | tf_op jit(solution)/shard_map/ppermute | solution.py:72
  63.3 17.5 %collective-permute-start.3 = (f32[3,4,896]{2,1,0:T(4,128)S(1)}, f32[3,4,896]{2,1,0:T(4,128)S(1)}, u32[]{:S(2)}, u32[]{:S(2)}) collective-permute-start(f32[3,4,896]{2,1,0:T(4,128)S(1)} %get-tuple-element.34), channel_id=1, source_target_pairs={{8,0},{16,8},{24,16},{32,24},{40,32},{48,40},{56,48},{64,56},{72,6... | collective-permute-start | bytes 129032 | tf_op jit(solution)/shard_map/ppermute | solution.py:73
  80.8 3.6 %collective-permute-start.4 = (f32[3,24,4]{2,1,0:T(8,128)S(1)}, f32[3,24,4]{2,1,0:T(8,128)S(1)}, u32[]{:S(2)}, u32[]{:S(2)}) collective-permute-start(f32[3,24,4]{2,1,0:T(8,128)S(1)} %get-tuple-element.25), channel_id=1, source_target_pairs={{0,1},{1,2},{2,3},{3,4},{4,5},{5,6},{6,7},{7,0},{8,9},{9,10},{10,1... | collective-permute-start | bytes 3464 | tf_op jit(solution)/shard_map/ppermute | solution.py:72
  83.4 3.7 %collective-permute-start.5 = (f32[3,24,4]{2,1,0:T(8,128)S(1)}, f32[3,24,4]{2,1,0:T(8,128)S(1)}, u32[]{:S(2)}, u32[]{:S(2)}) collective-permute-start(f32[3,24,4]{2,1,0:T(8,128)S(1)} %get-tuple-element.26), channel_id=1, source_target_pairs={{1,0},{2,1},{3,2},{4,3},{5,4},{6,5},{7,6},{0,7},{9,8},{10,9},{11,1... | collective-permute-start | bytes 3464 | tf_op jit(solution)/shard_map/ppermute | solution.py:73
  87.8 9.2 %collective-permute-start.6 = (f32[3,4,896]{2,1,0:T(4,128)S(1)}, f32[3,4,896]{2,1,0:T(4,128)S(1)}, u32[]{:S(2)}, u32[]{:S(2)}) collective-permute-start(f32[3,4,896]{2,1,0:T(4,128)S(1)} %get-tuple-element.31), channel_id=1, source_target_pairs={{0,8},{8,16},{16,24},{24,32},{32,40},{40,48},{48,56},{56,64},{64,7... | collective-permute-start | bytes 129032 | tf_op jit(solution)/shard_map/ppermute | solution.py:72
  89.7 8.4 %collective-permute-start.7 = (f32[3,4,896]{2,1,0:T(4,128)S(1)}, f32[3,4,896]{2,1,0:T(4,128)S(1)}, u32[]{:S(2)}, u32[]{:S(2)}) collective-permute-start(f32[3,4,896]{2,1,0:T(4,128)S(1)} %get-tuple-element.32), channel_id=1, source_target_pairs={{8,0},{16,8},{24,16},{32,24},{40,32},{48,40},{56,48},{64,56},{72,6... | collective-permute-start | bytes 129032 | tf_op jit(solution)/shard_map/ppermute | solution.py:73
  98.2 2.3 %collective-permute-start.8 = (f32[3,24,4]{2,1,0:T(8,128)S(1)}, f32[3,24,4]{2,1,0:T(8,128)S(1)}, u32[]{:S(2)}, u32[]{:S(2)}) collective-permute-start(f32[3,24,4]{2,1,0:T(8,128)S(1)} %get-tuple-element.23), channel_id=1, source_target_pairs={{0,1},{1,2},{2,3},{3,4},{4,5},{5,6},{6,7},{7,0},{8,9},{9,10},{10,1... | collective-permute-start | bytes 3464 | tf_op jit(solution)/shard_map/ppermute | solution.py:72
  98.8 3.4 %collective-permute-start.9 = (f32[3,24,4]{2,1,0:T(8,128)S(1)}, f32[3,24,4]{2,1,0:T(8,128)S(1)}, u32[]{:S(2)}, u32[]{:S(2)}) collective-permute-start(f32[3,24,4]{2,1,0:T(8,128)S(1)} %get-tuple-element.24), channel_id=1, source_target_pairs={{1,0},{2,1},{3,2},{4,3},{5,4},{6,5},{7,6},{0,7},{9,8},{10,9},{11,1... | collective-permute-start | bytes 3464 | tf_op jit(solution)/shard_map/ppermute | solution.py:73
  102.9 9.2 %collective-permute-start.10 = (f32[3,4,896]{2,1,0:T(4,128)S(1)}, f32[3,4,896]{2,1,0:T(4,128)S(1)}, u32[]{:S(2)}, u32[]{:S(2)}) collective-permute-start(f32[3,4,896]{2,1,0:T(4,128)S(1)} %get-tuple-element.29), channel_id=1, source_target_pairs={{0,8},{8,16},{16,24},{24,32},{32,40},{40,48},{48,56},{56,64},{64,7... | collective-permute-start | bytes 129032 | tf_op jit(solution)/shard_map/ppermute | solution.py:72
  104.8 8.4 %collective-permute-start.11 = (f32[3,4,896]{2,1,0:T(4,128)S(1)}, f32[3,4,896]{2,1,0:T(4,128)S(1)}, u32[]{:S(2)}, u32[]{:S(2)}) collective-permute-start(f32[3,4,896]{2,1,0:T(4,128)S(1)} %get-tuple-element.30), channel_id=1, source_target_pairs={{8,0},{16,8},{24,16},{32,24},{40,32},{48,40},{56,48},{64,56},{72,6... | collective-permute-start | bytes 129032 | tf_op jit(solution)/shard_map/ppermute | solution.py:73
  113.3 3.8 %collective-permute-start.12 = (f32[3,24,4]{2,1,0:T(8,128)S(1)}, f32[3,24,4]{2,1,0:T(8,128)S(1)}, u32[]{:S(2)}, u32[]{:S(2)}) collective-permute-start(f32[3,24,4]{2,1,0:T(8,128)S(1)} %get-tuple-element.21), channel_id=1, source_target_pairs={{0,1},{1,2},{2,3},{3,4},{4,5},{5,6},{6,7},{7,0},{8,9},{9,10},{10,1... | collective-permute-start | bytes 3464 | tf_op jit(solution)/shard_map/ppermute | solution.py:72
  114.2 3.4 %collective-permute-start.13 = (f32[3,24,4]{2,1,0:T(8,128)S(1)}, f32[3,24,4]{2,1,0:T(8,128)S(1)}, u32[]{:S(2)}, u32[]{:S(2)}) collective-permute-start(f32[3,24,4]{2,1,0:T(8,128)S(1)} %get-tuple-element.22), channel_id=1, source_target_pairs={{1,0},{2,1},{3,2},{4,3},{5,4},{6,5},{7,6},{0,7},{9,8},{10,9},{11,1... | collective-permute-start | bytes 3464 | tf_op jit(solution)/shard_map/ppermute | solution.py:73
  118.3 9.2 %collective-permute-start.14 = (f32[3,4,896]{2,1,0:T(4,128)S(1)}, f32[3,4,896]{2,1,0:T(4,128)S(1)}, u32[]{:S(2)}, u32[]{:S(2)}) collective-permute-start(f32[3,4,896]{2,1,0:T(4,128)S(1)} %get-tuple-element.27), channel_id=1, source_target_pairs={{0,8},{8,16},{16,24},{24,32},{32,40},{40,48},{48,56},{56,64},{64,7... | collective-permute-start | bytes 129032 | tf_op jit(solution)/shard_map/ppermute | solution.py:72
  120.2 8.4 %collective-permute-start.15 = (f32[3,4,896]{2,1,0:T(4,128)S(1)}, f32[3,4,896]{2,1,0:T(4,128)S(1)}, u32[]{:S(2)}, u32[]{:S(2)}) collective-permute-start(f32[3,4,896]{2,1,0:T(4,128)S(1)} %get-tuple-element.28), channel_id=1, source_target_pairs={{8,0},{16,8},{24,16},{32,24},{40,32},{48,40},{56,48},{64,56},{72,6... | collective-permute-start | bytes 129032 | tf_op jit(solution)/shard_map/ppermute | solution.py:73
  128.7 5.0 %collective-permute-start.16 = (f32[3,24,4]{2,1,0:T(8,128)S(1)}, f32[3,24,4]{2,1,0:T(8,128)S(1)}, u32[]{:S(2)}, u32[]{:S(2)}) collective-permute-start(f32[3,24,4]{2,1,0:T(8,128)S(1)} %get-tuple-element.19), channel_id=1, source_target_pairs={{0,1},{1,2},{2,3},{3,4},{4,5},{5,6},{6,7},{7,0},{8,9},{9,10},{10,1... | collective-permute-start | bytes 3464 | tf_op jit(solution)/shard_map/ppermute | solution.py:72
  129.5 4.3 %collective-permute-start.17 = (f32[3,24,4]{2,1,0:T(8,128)S(1)}, f32[3,24,4]{2,1,0:T(8,128)S(1)}, u32[]{:S(2)}, u32[]{:S(2)}) collective-permute-start(f32[3,24,4]{2,1,0:T(8,128)S(1)} %get-tuple-element.20), channel_id=1, source_target_pairs={{1,0},{2,1},{3,2},{4,3},{5,4},{6,5},{7,6},{0,7},{9,8},{10,9},{11,1... | collective-permute-start | bytes 3464 | tf_op jit(solution)/shard_map/ppermute | solution.py:73
where the time goes:
time: 151 us; the launch traced here: 150 us
  starting transfers between devices  83.7 us (55%)
  other arithmetic  29.4 us (19%)
  waiting for transfers between devices  17.7 us (12%)
  blocking collectives  16.3 us (11%)
  local copies, waits for them, and re-layouts  2.06 us (1%)
    ppermute x8, starting transfers between devices, extended(): after = lax.ppermute(leading, axis, down)  45 us
    reduce_sum x1, other arithmetic, body(): sums = jnp.sum(layer * starred, axis=2)  15.3 us
    ppermute x8, starting transfers between devices, extended(): before = lax.ppermute(last, axis, up)  14.6 us
    ppermute x1, starting transfers between devices, with_halo(): lax.ppermute(leading, axis, [(b, a) for a, b in up])  12.9 us
    all_to_all x1, blocking collectives, body(): lax.all_to_all(changes, SUB, split_axis=1, concat_axis=2, tiled=True)  12.8 us
    ppermute x8, waiting for transfers between devices, extended(): after = lax.ppermute(leading, axis, down)  9.19 us
    all_to_all x1, starting transfers between devices, moved_by_axis(): out = lax.all_to_all(out, axes[k], k, k, tiled=True)  6.65 us
    another operation x6, other arithmetic, body(): paired = jnp.stack((east, north))  5.76 us
  transfers between devices with their start and end apart: 19, of which 14 were waited for; matrix products, arithmetic and copies ran while one was open for 4% of the time, Pallas kernels for 0%

commit v1 on v0

v1 whole, which is shorter than its diff:
```python
import functools

import jax
import jax.numpy as jnp
from jax import lax
from jax.experimental import pallas as pl
from jax.experimental.pallas import tpu as pltpu
from jax.sharding import PartitionSpec as P

MESH = pl.DeviceIdType.MESH
T = 128
NSUB = 4
viscosity = 0.05
mixing = 0.1
rotation = 0.2
continuity = 0.5
pressure = 0.5


def up8(n):
    return (n + 7) // 8 * 8


def tiles_of(value):
    return [value[:, t * T : (t + 1) * T] for t in range(value.shape[1] // T)]


def shift_lanes(x, by):
    return pltpu.roll(x, by % x.shape[1], 1)


def shift_rows(x, by):
    return pltpu.roll(x, by % x.shape[0], 0)


def ring_extended(x):
    w = x.shape[1]
    return jnp.concatenate([shift_rows(x[:, w - T :], 1), x, shift_rows(x[:, :T], -1)], axis=1)


def dx12(q):
    return shift_lanes(q, 2) - shift_lanes(q, -2) + 8.0 * (shift_lanes(q, -1) - shift_lanes(q, 1))


def dy12(q0, q1):
    u0, u1 = shift_rows(q0, -1), shift_rows(q1, -1)
    d0, d1 = shift_rows(q0, 1), shift_rows(q1, 1)
    return d0 - u0 + 8.0 * (q1 - d1), d1 - u1 + 8.0 * (u0 - q0)


def kernel(
    NB, NS, K, NL,
    thick, cor, e_hbm, n_hbm, l_hbm, h_hbm,
    eo_hbm, no_hbm, so_hbm,
    ein, nin, lin, hin, lev, M, RP, RN, ST, fs, fr, ds_, dr, B, G, cs, cr, X, inv, eo, no, so,
    in_sem, h_sem, bulk_sem, a2a_sem, z_sem, x_sem, out_sem,
):
    W = NL // NS
    TT = W // T
    L = W + 2 * T
    QF, QD, QC = up8((TT + 2) * 4), up8((TT + 2) * 2), up8(TT * 4)
    PK = 2 * NL // T
    b = lax.axis_index("blk")
    s = lax.axis_index("sub")
    flat = b * NS + s
    total = NB * NS
    prev = lax.rem(flat + total - 1, total)
    nxt = lax.rem(flat + 1, total)
    prev = (lax.div(prev, NS), lax.rem(prev, NS))
    nxt = (lax.div(nxt, NS), lax.rem(nxt, NS))
    zup = (lax.rem(b + 1, NB), s)
    zdn = (lax.rem(b + NB - 1, NB), s)
    peers = [(b, lax.rem(s + j, NS)) for j in range(1, NS)]

    loads = [
        pltpu.make_async_copy(l_hbm, lin, in_sem.at[0]),
        pltpu.make_async_copy(e_hbm, ein, in_sem.at[1]),
        pltpu.make_async_copy(n_hbm, nin, in_sem.at[2]),
    ]
    h_loads = [
        pltpu.make_async_copy(
            h_hbm.at[:, pl.ds(t * T, T)], hin.at[pl.ds(t * 16, 16), :], h_sem.at[t]
        )
        for t in range(TT)
    ]
    for c in loads + h_loads:
        c.start()
    barrier = pltpu.get_barrier_semaphore()
    for peer in [prev, nxt, zup, zdn] + peers:
        pl.semaphore_signal(barrier, inc=1, device_id=peer, device_id_type=MESH)

    loads[0].wait()
    levs = []
    for r in range(2):
        v = jnp.concatenate([lin[pl.ds(t * 2 + r, 8, stride=2 * TT), :] for t in range(TT)], axis=1)
        lev[r] = v
        levs.append(v)
    for r in range(2):
        acc = jnp.zeros((8, W), jnp.float32)
        for k in range(K):
            acc = acc + jnp.where(levs[r] > k, thick[k], 0.0)
        inv[r] = jnp.where(levs[r] > 0, 1.0 / jnp.where(levs[r] > 0, acc, 1.0), 0.0)
        ext = ring_extended(acc)
        for t, v in enumerate(tiles_of(ext)):
            ds_[pl.ds(t * 2 + r, 8, stride=QD), :] = v
    for c in h_loads:
        c.wait()
    for r in range(2):
        for t in range(TT):
            G[0, r, 8:16, (t + 1) * T : (t + 2) * T] = hin[pl.ds(t * 16 + r, 8, stride=2), :]
    loads[1].wait()
    loads[2].wait()

    def mask_level(k, _):
        for r in range(2):
            wet = lev[r] > k
            for f, src in ((0, ein), (1, nin)):
                v = jnp.concatenate(
                    [src[pl.ds(k * PK + t * 2 + r, 8, stride=2 * TT), :] for t in range(TT)], axis=1
                )
                M[k, f, r] = jnp.where(wet, v, 0.0)
        return 0

    lax.fori_loop(0, K, mask_level, 0)

    pl.semaphore_wait(barrier, 4 + NS - 1)

    def a2a(src, dst, q, which):
        out = []
        for j in range(1, NS):
            to = lax.rem(s + j, NS)
            out.append(
                pltpu.make_async_remote_copy(
                    src_ref=src.at[pl.ds(pl.multiple_of(to * q, 8), q), :],
                    dst_ref=dst.at[pl.ds(pl.multiple_of(s * q, 8), q), :],
                    send_sem=a2a_sem.at[which, 0, j - 1],
                    recv_sem=a2a_sem.at[which, 1, j - 1],
                    device_id=(b, to),
                    device_id_type=MESH,
                )
            )
        return out

    def own(src, dst, q):
        at = pl.ds(pl.multiple_of(s * q, 8), q)
        dst[at, :] = src[at, :]

    d_copies = a2a(ds_, dr, QD, 0)
    for c in d_copies:
        c.start()
    right, left = (b, lax.rem(s + 1, NS)), (b, lax.rem(s + NS - 1, NS))
    h_copies = [
        pltpu.make_async_remote_copy(
            src_ref=G.at[0, :, pl.ds(8, 8), pl.ds(at, T)],
            dst_ref=G.at[0, :, pl.ds(8, 8), pl.ds(to, T)],
            send_sem=x_sem.at[0, i],
            recv_sem=x_sem.at[1, i],
            device_id=peer,
            device_id_type=MESH,
        )
        for i, (at, to, peer) in enumerate(((W, 0, right), (T, W + T, left)))
    ]
    for c in h_copies:
        c.start()

    def bulk(k, way):
        return pltpu.make_async_remote_copy(
            src_ref=M.at[k],
            dst_ref=(RN if way == 0 else RP).at[k],
            send_sem=bulk_sem.at[way, 0, k],
            recv_sem=bulk_sem.at[way, 1, k],
            device_id=prev if way == 0 else nxt,
            device_id_type=MESH,
        )

    def start_bulk(k, _):
        bulk(k, 0).start()
        bulk(k, 1).start()
        return 0

    lax.fori_loop(0, K, start_bulk, 0)
    own(ds_, dr, QD)

    cv = viscosity / 12.0

    def local_level(k, _):
        above = jnp.maximum(k - 1, 0)
        below = jnp.minimum(k + 1, K - 1)
        for r in range(2):
            turn = rotation * cor[r]
            for f in range(2):
                x = M[k, f, r]
                ext = ring_extended(x)
                near = (shift_lanes(ext, 1) + shift_lanes(ext, -1))[:, T : T + W] + M[k, f, 1 - r]
                far = (shift_lanes(ext, 2) + shift_lanes(ext, -2))[:, T : T + W]
                lap = 16.0 * near - far
                vz = M[above, f, r] + M[below, f, r]
                other = M[k, 1 - f, r]
                sign = turn if f == 0 else -turn
                ST[k, f, r] = (1.0 - 60.0 * cv - 2.0 * mixing) * x + cv * lap + mixing * vz + sign * other
        return 0

    lax.fori_loop(0, K, local_level, 0)

    for c in d_copies:
        c.wait_recv()
    for c in h_copies:
        c.wait_recv()
    for r in range(2):
        for t in range(TT + 2):
            G[1, r, 8:16, t * T : (t + 1) * T] = dr[pl.ds(t * 2 + r, 8, stride=QD), :]

    def zcopies(buf, which):
        return [
            pltpu.make_async_remote_copy(
                src_ref=buf.at[:, :, pl.ds(8, 8), :],
                dst_ref=buf.at[:, :, pl.ds(to, 8), :],
                send_sem=z_sem.at[which, 0, i],
                recv_sem=z_sem.at[which, 1, i],
                device_id=peer,
                device_id_type=MESH,
            )
            for i, (to, peer) in enumerate(((0, zup), (16, zdn)))
        ]

    g_copies = zcopies(G, 0)
    for c in g_copies:
        c.start()

    gp = jnp.where(flat > 0, cv, 0.0)
    gn = jnp.where(flat < total - 1, cv, 0.0)

    def finish_level(k, sums):
        bulk(k, 0).wait_recv()
        bulk(k, 1).wait_recv()
        th = thick[k]
        out = []
        for f in range(2):
            p0, p1 = RP[k, f, 0], RP[k, f, 1]
            n0, n1 = RN[k, f, 0], RN[k, f, 1]
            for r in range(2):
                if r == 0:
                    add = gp * (16.0 * p1 - p0) - gn * n0
                else:
                    add = gn * (16.0 * n0 - n1) - gp * p1
                v = jnp.where(lev[r] > k, ST[k, f, r] + add, 0.0)
                ST[k, f, r] = v
                out.append(sums[2 * f + r] + th * v)
        return tuple(out)

    sums = lax.fori_loop(0, K, finish_level, tuple(jnp.zeros((8, W), jnp.float32) for _ in range(4)))
    for f in range(2):
        for r in range(2):
            for t, v in enumerate(tiles_of(ring_extended(sums[2 * f + r]))):
                fs[pl.ds(t * 4 + f * 2 + r, 8, stride=QF), :] = v
    f_copies = a2a(fs, fr, QF, 1)
    for c in f_copies:
        c.start()
    own(fs, fr, QF)
    for c in f_copies:
        c.wait_recv()
    for f in range(2):
        for r in range(2):
            for t in range(TT + 2):
                B[f, r, 8:16, t * T : (t + 1) * T] = fr[pl.ds(t * 4 + f * 2 + r, 8, stride=QF), :]
    b_copies = zcopies(B, 1)
    for c in b_copies:
        c.start()
    for c in g_copies:
        c.wait_recv()
    for c in b_copies:
        c.wait_recv()

    row = lax.broadcasted_iota(jnp.int32, (24, T), 0)
    inside = jnp.logical_and(
        jnp.logical_or(row >= 8, b > 0), jnp.logical_or(row < 16, b < NB - 1)
    )
    inside = jnp.concatenate([inside.astype(jnp.float32)] * (TT + 2), axis=1)
    east = [B[0, r] for r in range(2)]
    north = [jnp.where(inside > 0.0, B[1, r], 0.0) for r in range(2)]
    high = [jnp.where(inside > 0.0, G[0, r], 0.0) for r in range(2)]
    deep = [jnp.where(inside > 0.0, G[1, r], 0.0) * (pressure / 12.0) for r in range(2)]
    step = inside * (continuity / 12.0)
    for _ in range(NSUB):
        dn = dy12(north[0], north[1])
        high = [high[r] - step * (dx12(east[r]) + dn[r]) for r in range(2)]
        dh = dy12(high[0], high[1])
        east = [east[r] - deep[r] * dx12(high[r]) for r in range(2)]
        north = [north[r] - deep[r] * dh[r] for r in range(2)]
    for f, field in ((0, east), (1, north)):
        for r in range(2):
            change = field[r][8:16, T : T + W] - B[f, r, 8:16, T : T + W]
            for t, v in enumerate(tiles_of(change)):
                cs[pl.ds(t * 4 + f * 2 + r, 8, stride=QC), :] = v
    c_copies = a2a(cs, cr, QC, 2)
    for c in c_copies:
        c.start()
    for r in range(2):
        for t in range(TT):
            so[pl.ds(t * 16 + r, 8, stride=2), :] = high[r][8:16, (t + 1) * T : (t + 2) * T]
    so_copies = [
        pltpu.make_async_copy(
            so.at[pl.ds(t * 16, 16), :], so_hbm.at[:, pl.ds(t * T, T)], h_sem.at[t]
        )
        for t in range(TT)
    ]
    for c in so_copies:
        c.start()
    own(cs, cr, QC)
    for c in c_copies:
        c.wait_recv()
    for f in range(2):
        for r in range(2):
            v = jnp.concatenate(
                [cr[pl.ds(t * 4 + f * 2 + r, 8, stride=QC), :] for t in range(TT)], axis=1
            )
            X[f, r] = v * inv[r]

    def store_level(k, _):
        for r in range(2):
            wet = lev[r] > k
            for f, dst in ((0, eo), (1, no)):
                v = ST[k, f, r] + jnp.where(wet, X[f, r], 0.0)
                for t in range(TT):
                    dst[pl.ds(k * PK + t * 2 + r, 8, stride=2 * TT), :] = v[:, t * T : (t + 1) * T]
        return 0

    lax.fori_loop(0, K, store_level, 0)
    outs = [
        pltpu.make_async_copy(eo, eo_hbm, out_sem.at[0]),
        pltpu.make_async_copy(no, no_hbm, out_sem.at[1]),
    ]
    for c in outs:
        c.start()

    def drain(k, _):
        bulk(k, 0).wait_send()
        bulk(k, 1).wait_send()
        return 0

    lax.fori_loop(0, K, drain, 0)
    for c in d_copies + h_copies + f_copies + g_copies + b_copies + c_copies:
        c.wait_send()
    for c in outs + so_copies:
        c.wait()


def flattened(x):
    k = x.shape[1]
    x = x.reshape(2, k, -1, T).transpose(1, 2, 0, 3)
    return x.reshape(-1, T)


def unflattened(x, k):
    x = x.reshape(k, -1, 2, T).transpose(2, 0, 1, 3)
    return x.reshape(2, k, -1)


def body(NB, NS, east_flow, north_flow, levels, coriolis, thickness, surface):
    _, K, NL = east_flow.shape
    W = NL // NS
    TT = W // T
    L = W + 2 * T
    rows = K * 2 * NL // T
    QF, QD, QC = up8((TT + 2) * 4), up8((TT + 2) * 2), up8(TT * 4)
    f32 = jnp.float32
    lev = levels.reshape(2, -1, T).transpose(1, 0, 2).reshape(-1, T)
    any_ = pl.BlockSpec(memory_space=pl.ANY)
    smem = pl.BlockSpec(memory_space=pltpu.SMEM)
    big = pltpu.VMEM((K, 2, 2, 8, W), f32)
    dma = pltpu.SemaphoreType.DMA
    eo, no, so = pl.pallas_call(
        functools.partial(kernel, NB, NS, K, NL),
        out_shape=(
            jax.ShapeDtypeStruct((rows, T), f32),
            jax.ShapeDtypeStruct((rows, T), f32),
            jax.ShapeDtypeStruct((16, W), f32),
        ),
        in_specs=[smem, smem, any_, any_, any_, any_],
        out_specs=[any_, any_, any_],
        scratch_shapes=[
            pltpu.VMEM((rows, T), f32),
            pltpu.VMEM((rows, T), f32),
            pltpu.VMEM((2 * NL // T, T), jnp.int32),
            pltpu.VMEM((16 * TT, T), f32),
            pltpu.VMEM((2, 8, W), jnp.int32),
            big,
            big,
            big,
            big,
            pltpu.VMEM((NS * QF, T), f32),
            pltpu.VMEM((NS * QF, T), f32),
            pltpu.VMEM((NS * QD, T), f32),
            pltpu.VMEM((NS * QD, T), f32),
            pltpu.VMEM((2, 2, 24, L), f32),
            pltpu.VMEM((2, 2, 24, L), f32),
            pltpu.VMEM((NS * QC, T), f32),
            pltpu.VMEM((NS * QC, T), f32),
            pltpu.VMEM((2, 2, 8, W), f32),
            pltpu.VMEM((2, 8, W), f32),
            pltpu.VMEM((rows, T), f32),
            pltpu.VMEM((rows, T), f32),
            pltpu.VMEM((16 * TT, T), f32),
            dma((3,)),
            dma((TT,)),
            dma((2, 2, K)),
            dma((3, 2, NS - 1)),
            dma((2, 2, 2)),
            dma((2, 2)),
            dma((2,)),
        ],
        compiler_params=pltpu.CompilerParams(collective_id=0, has_side_effects=True),
    )(thickness, coriolis, flattened(east_flow), flattened(north_flow), lev, surface)
    return unflattened(eo, K), unflattened(no, K), so


def solution(mesh):
    NB, NS = mesh.shape["blk"], mesh.shape["sub"]
    both = ("blk", "sub")
    return jax.shard_map(
        functools.partial(body, NB, NS),
        mesh=mesh,
        in_specs=(P(both, None, None), P(both, None, None), P(both, None), P(both), P(), P("blk", "sub")),
        out_specs=(P(both, None, None), P(both, None, None), P("blk", "sub")),
        check_vma=False,
    )
```

time: 151 us -> 68.3 us (0.45)
  starting transfers between devices: 83.7 us -> 0 us
  Pallas kernels: 0 us -> 63.9 us
  other arithmetic: 29.4 us -> 0 us
  waiting for transfers between devices: 17.7 us -> 0 us
  blocking collectives: 16.3 us -> 0 us
    ppermute x18 -> x0, starting transfers between devices: 77 us -> none  [the longest x8 45 us: extended(): after = lax.ppermute(leading, axis, down)]
    pallas_call x0 -> x1, Pallas kernels: none -> 63.9 us  [body(): pl.pallas_call(functools.partial(kernel, NB, NS, K, NL), out_shape=(jax.S...]
    reduce_sum x2 -> x0, other arithmetic: 17.5 us -> none  [the longest x1 15.3 us: body(): sums = jnp.sum(layer * starred, axis=2)]
    all_to_all x2 -> x0, blocking collectives: 16.3 us -> none  [the longest x1 12.8 us: body(): lax.all_to_all(changes, SUB, split_axis=1, concat_axis=2, tiled=True)]
    ppermute x18 -> x0, waiting for transfers between devices: 12.7 us -> none  [the longest x8 9.19 us: extended(): after = lax.ppermute(leading, axis, down)]
    all_to_all x1 -> x0, starting transfers between devices: 6.65 us -> none  [moved_by_axis(): out = lax.all_to_all(out, axes[k], k, k, tiled=True)]
    another operation x7 -> x0, other arithmetic: 6.57 us -> none  [the longest x6 5.76 us: body(): paired = jnp.stack((east, north))]
    all_to_all x1 -> x0, waiting for transfers between devices: 5.06 us -> none  [moved_by_axis(): out = lax.all_to_all(out, axes[k], k, k, tiled=True)]
  transfers between devices with their start and end apart: 19 -> 0, of which waited for: 14 -> 0; matrix products, arithmetic and copies ran while one was open for 4% -> 0% of each run, Pallas kernels for 0% -> 0%
where the time goes in v1:
time: 68.3 us; the launch traced here: 68.1 us
  Pallas kernels  63.9 us (94%)
  local copies, waits for them, and re-layouts  3.54 us (5%)
    pallas_call x1, Pallas kernels, body(): pl.pallas_call(functools.partial(kernel, NB, NS, K, NL), out_shape=(jax.S...  63.9 us
    unnamed x7, local copies, waits for them, and re-layouts  3.54 us

profile of v1, /device:TPU:1, one launch (start us, length us, event | category | flops | bytes accessed | tf_op | source)
XLA Modules:
  0.0 68.1 jit_solution(11287812262642950100)
XLA Ops:
  0.6 63.9 %shard_map.85 = (f32[1344,128]{1,0:T(8,128)}, f32[1344,128]{1,0:T(8,128)}, f32[16,896]{1,0:T(8,128)}) custom-call(f32[12]{0:T(128)} %thick.1, f32[2]{0:T(128)} %cor.1, f32[1344,128]{1,0:T(8,128)} %bitcast.25, f32[1344,128]{1,0:T(8,128)} %bitcast.26, s32[112,128]{1,0:T(8,128)} %bitcast.29, f32[16,896]{1,0:T(8,128)} %h_hbm.1), custom_call_target="tpu_custom_call" | custom-call | tf_op jit(solution)/shard_map/pallas_call | solution.py:372
  64.5 0.0 copy-start
  64.6 2.1 %copy.17 = f32[2,12,7168]{2,0,1:T(2,128)} copy(f32[2,12,7168]{2,0,1:T(2,128)} %bitcast.28) | data formatting | bytes 1376256
  66.6 0.0 copy-done
  66.6 0.0 copy-start.1
  66.6 0.8 %copy.18 = f32[2,12,7168]{2,0,1:T(2,128)} copy(f32[2,12,7168]{2,0,1:T(2,128)S(1)} %bitcast.27) | data formatting | bytes 1376256
  67.5 0.0 copy-done.1
  67.5 0.6 copy.19
Async XLA Ops:
  64.5 2.1 %copy-start = (f32[1344,128]{1,0:T(8,128)S(1)}, f32[1344,128]{1,0:T(8,128)}, u32[]{:S(2)}) copy-start(f32[1344,128]{1,0:T(8,128)} %get-tuple-element.7) | copy-start | bytes 2064388
  66.6 0.9 %copy-start.1 = (f32[16,896]{1,0:T(8,128)S(1)}, f32[16,896]{1,0:T(8,128)}, u32[]{:S(2)}) copy-start(f32[16,896]{1,0:T(8,128)} %get-tuple-element.14) | copy-start | bytes 172036

commit v2 on v1

v2 whole, which is shorter than its diff:
```python
import functools

import jax
import jax.numpy as jnp
from jax import lax
from jax.experimental import pallas as pl
from jax.experimental.pallas import tpu as pltpu
from jax.sharding import PartitionSpec as P

MESH = pl.DeviceIdType.MESH
T = 128
NSUB = 4
VMEM_LIMIT = 16 << 20
B1, B2, B3 = 3, 6, 10
F2 = 4
FAR_FIRST = (4, 3, 5, 2, 6, 1, 7)
viscosity = 0.05
mixing = 0.1
rotation = 0.2
continuity = 0.5
pressure = 0.5


def up8(n):
    return (n + 7) // 8 * 8


def tiles_of(value):
    return [value[:, t * T : (t + 1) * T] for t in range(value.shape[1] // T)]


def shift_lanes(x, by):
    return pltpu.roll(x, by % x.shape[1], 1)


def shift_rows(x, by):
    return pltpu.roll(x, by % x.shape[0], 0)


def ring_extended(x):
    w = x.shape[1]
    return with_rim(x, shift_rows(x[:, w - T :], 1), shift_rows(x[:, :T], -1))


def with_rim(x, before, after):
    low = lax.broadcasted_iota(jnp.int32, before.shape, 1) < T // 2
    return jnp.concatenate([x, jnp.where(low, after, before)], axis=1)


def dx12(q):
    return shift_lanes(q, 2) - shift_lanes(q, -2) + 8.0 * (shift_lanes(q, -1) - shift_lanes(q, 1))


def dy12(q0, q1):
    u0, u1 = shift_rows(q0, -1), shift_rows(q1, -1)
    d0, d1 = shift_rows(q0, 1), shift_rows(q1, 1)
    return d0 - u0 + 8.0 * (q1 - d1), d1 - u1 + 8.0 * (u0 - q0)


def kernel(
    NB, NS, K, NL,
    t_hbm, c_hbm, e_hbm, n_hbm, l_hbm, h_hbm,
    eo, no, so,
    thick, cor, ein, nin, lin, hin, lev, M, RP, RN, ST, fs, fr, ds_, dr, B, G, HX, cs, cr, X, inv,
    LP, LN, levx, PP, PN, QP, QN,
    in_sem, h_sem, bulk_sem, a2a_sem, z_sem, x_sem, n_sem,
):
    W = NL // NS
    TT = W // T
    L = W + T
    QF, QD, QC = up8((TT + 1) * 4), up8((TT + 1) * 2), up8(TT * 4)
    PK = 2 * NL // T
    b = lax.axis_index("blk")
    s = lax.axis_index("sub")
    flat = b * NS + s
    total = NB * NS
    prev = lax.rem(flat + total - 1, total)
    nxt = lax.rem(flat + 1, total)
    prev = (lax.div(prev, NS), lax.rem(prev, NS))
    nxt = (lax.div(nxt, NS), lax.rem(nxt, NS))
    zup = (lax.rem(b + 1, NB), s)
    zdn = (lax.rem(b + NB - 1, NB), s)
    peers = [(b, lax.rem(s + j, NS)) for j in range(1, NS)]
    has_prev, has_next = flat > 0, flat < total - 1
    has_dn, has_up = b > 0, b < NB - 1
    one = lambda there: jnp.where(there, 1, 0)

    loads = [
        pltpu.make_async_copy(l_hbm, lin, in_sem.at[0]),
        pltpu.make_async_copy(e_hbm, ein, in_sem.at[1]),
        pltpu.make_async_copy(n_hbm, nin, in_sem.at[2]),
        pltpu.make_async_copy(t_hbm, thick, in_sem.at[3]),
        pltpu.make_async_copy(c_hbm, cor, in_sem.at[4]),
    ]
    h_loads = [
        pltpu.make_async_copy(
            h_hbm.at[:, pl.ds(t * T, T)], hin.at[pl.ds(t * 16, 16), :], h_sem.at[t]
        )
        for t in range(TT)
    ]
    for c in loads + h_loads:
        c.start()
    barrier = pltpu.get_barrier_semaphore()
    for peer in peers:
        pl.semaphore_signal(barrier, inc=1, device_id=peer, device_id_type=MESH)
    for there, peer in ((has_prev, prev), (has_next, nxt), (has_dn, zdn), (has_up, zup)):

        @pl.when(there)
        def _():
            pl.semaphore_signal(barrier, inc=1, device_id=peer, device_id_type=MESH)


    def clear(there, refs):
        @pl.when(jnp.logical_not(there))
        def _():
            for ref in refs:
                ref[...] = jnp.zeros(ref.shape, ref.dtype)

    clear(has_prev, [QP, LP])
    clear(has_next, [QN, LN])
    clear(has_dn, [ref.at[i, j, pl.ds(0, 8)] for ref in (B, G) for i in range(2) for j in range(2)])
    clear(has_up, [ref.at[i, j, pl.ds(16, 8)] for ref in (B, G) for i in range(2) for j in range(2)])
    for there, buf in ((has_prev, RP), (has_next, RN)):

        @pl.when(jnp.logical_not(there))
        def _():
            def zero_level(k, _):
                for f in range(2):
                    for r in range(2):
                        buf[k, f, r] = jnp.zeros((8, W), jnp.float32)
                return 0

            lax.fori_loop(0, K, zero_level, 0)

    pl.semaphore_wait(barrier, NS - 1 + one(has_prev) + one(has_next) + one(has_dn) + one(has_up))

    def to_neighbours(src_up, src_down, dst_from_prev, dst_from_next, which):
        return [
            (
                out,
                back,
                pltpu.make_async_remote_copy(
                    src_ref=src,
                    dst_ref=dst,
                    send_sem=n_sem.at[which, 0, i],
                    recv_sem=n_sem.at[which, 1, i],
                    device_id=peer,
                    device_id_type=MESH,
                ),
            )
            for i, (src, dst, peer, out, back) in enumerate(
                (
                    (src_up, dst_from_prev, nxt, has_next, has_prev),
                    (src_down, dst_from_next, prev, has_prev, has_next),
                )
            )
        ]

    def start_if(copies):
        for out, _, c in copies:
            pl.when(out)(c.start)

    def wait_recv_if(copies):
        for _, back, c in copies:
            pl.when(back)(c.wait_recv)

    def wait_send_if(copies):
        for out, _, c in copies:
            pl.when(out)(c.wait_send)

    l_copies = to_neighbours(l_hbm, l_hbm, LP, LN, 0)
    start_if(l_copies)

    def a2a(src, dst, q, which):
        out = []
        for j in FAR_FIRST:
            to = lax.rem(s + j, NS)
            out.append(
                pltpu.make_async_remote_copy(
                    src_ref=src.at[pl.ds(pl.multiple_of(to * q, 8), q), :],
                    dst_ref=dst.at[pl.ds(pl.multiple_of(s * q, 8), q), :],
                    send_sem=a2a_sem.at[which, 0, j - 1],
                    recv_sem=a2a_sem.at[which, 1, j - 1],
                    device_id=(b, to),
                    device_id_type=MESH,
                )
            )
        return out

    def own(src, dst, q):
        at = pl.ds(pl.multiple_of(s * q, 8), q)
        dst[at, :] = src[at, :]

    loads[0].wait()
    loads[3].wait()
    loads[4].wait()
    levs = []
    for r in range(2):
        v = jnp.concatenate([lin[pl.ds(t * 2 + r, 8, stride=2 * TT), :] for t in range(TT)], axis=1)
        lev[r] = v
        levs.append(v)
    for r in range(2):
        acc = jnp.zeros((8, W), jnp.float32)
        for k in range(K):
            acc = acc + jnp.where(levs[r] > k, thick[k], 0.0)
        inv[r] = jnp.where(levs[r] > 0, 1.0 / jnp.where(levs[r] > 0, acc, 1.0), 0.0)
        ext = ring_extended(acc)
        for t, v in enumerate(tiles_of(ext)):
            ds_[pl.ds(t * 2 + r, 8, stride=QD), :] = v
    for c in h_loads:
        c.wait()
    for r in range(2):
        for t in range(TT):
            G[0, r, 8:16, t * T : (t + 1) * T] = hin[pl.ds(t * 16 + r, 8, stride=2), :]
    d_copies = a2a(ds_, dr, QD, 0)
    for c in d_copies:
        c.start()
    right, left = (b, lax.rem(s + 1, NS)), (b, lax.rem(s + NS - 1, NS))
    h_copies = [
        pltpu.make_async_remote_copy(
            src_ref=G.at[0, :, pl.ds(8, 8), pl.ds(at, T)],
            dst_ref=HX.at[i],
            send_sem=x_sem.at[0, i],
            recv_sem=x_sem.at[1, i],
            device_id=peer,
            device_id_type=MESH,
        )
        for i, (at, peer) in enumerate(((W - T, right), (0, left)))
    ]
    for c in h_copies:
        c.start()
    loads[1].wait()
    loads[2].wait()

    def mask_level(k, _):
        for r in range(2):
            wet = lev[r] > k
            for f, src in ((0, ein), (1, nin)):
                v = jnp.concatenate(
                    [src[pl.ds(k * PK + t * 2 + r, 8, stride=2 * TT), :] for t in range(TT)], axis=1
                )
                M[k, f, r] = jnp.where(wet, v, 0.0)
        return 0

    lax.fori_loop(0, K, mask_level, 0)

    def bulk(k, way):
        return pltpu.make_async_remote_copy(
            src_ref=M.at[k],
            dst_ref=(RN if way == 0 else RP).at[k],
            send_sem=bulk_sem.at[way, 0, k],
            recv_sem=bulk_sem.at[way, 1, k],
            device_id=prev if way == 0 else nxt,
            device_id_type=MESH,
        )

    def start_bulk(first, last):
        for k in range(first, last):
            pl.when(has_prev)(bulk(k, 0).start)
            pl.when(has_next)(bulk(k, 1).start)

    start_bulk(0, B1)
    own(ds_, dr, QD)

    cv = viscosity / 12.0

    def local_level(k, sums):
        above = jnp.maximum(k - 1, 0)
        below = jnp.minimum(k + 1, K - 1)
        th = thick[k]
        out = []
        for f in range(2):
            for r in range(2):
                turn = rotation * cor[r]
                x = M[k, f, r]
                ext = ring_extended(x)
                near = (shift_lanes(ext, 1) + shift_lanes(ext, -1))[:, :W] + M[k, f, 1 - r]
                far = (shift_lanes(ext, 2) + shift_lanes(ext, -2))[:, :W]
                lap = 16.0 * near - far
                vz = M[above, f, r] + M[below, f, r]
                other = M[k, 1 - f, r]
                sign = turn if f == 0 else -turn
                v = (1.0 - 60.0 * cv - 2.0 * mixing) * x + cv * lap + mixing * vz + sign * other
                ST[k, f, r] = v
                out.append(sums[2 * f + r] + jnp.where(lev[r] > k, th * v, 0.0))
        return tuple(out)

    zeros = tuple(jnp.zeros((8, W), jnp.float32) for _ in range(4))
    sums = lax.fori_loop(0, K // 2, local_level, zeros)

    wait_recv_if(l_copies)
    for i, src in ((0, LP), (1, LN)):
        for r in range(2):
            levx[i, r] = jnp.concatenate(
                [src[pl.ds(t * 2 + r, 8, stride=2 * TT), :] for t in range(TT)], axis=1
            )

    def partial_level(i):
        def level(k, sums):
            th = thick[k]
            wet = [levx[i, r] > k for r in range(2)]
            out = []
            for f in range(2):
                m0, m1 = M[k, f, 0], M[k, f, 1]
                terms = (-m0, 16.0 * m0 - m1) if i == 0 else (16.0 * m1 - m0, -m1)
                for r in range(2):
                    out.append(sums[2 * f + r] + jnp.where(wet[r], th * terms[r], 0.0))
            return tuple(out)

        return level

    for i, dst in ((0, PP), (1, PN)):
        part = lax.fori_loop(0, K, partial_level(i), zeros)
        for f in range(2):
            for r in range(2):
                dst[f, r] = part[2 * f + r]
    p_copies = to_neighbours(PN, PP, QP, QN, 1)
    start_if(p_copies)
    start_bulk(B1, B2)
    sums = lax.fori_loop(K // 2, K, local_level, sums)

    for c in d_copies + h_copies:
        c.wait_recv()
    for r in range(2):
        G[0, r, 8:16, W:L] = with_rim(HX[1, r], HX[0, r], HX[1, r])[:, T:]
        for t in range(TT + 1):
            G[1, r, 8:16, t * T : (t + 1) * T] = dr[pl.ds(t * 2 + r, 8, stride=QD), :]

    def zcopies(buf, which):
        return [
            (
                out,
                back,
                pltpu.make_async_remote_copy(
                    src_ref=buf.at[:, :, pl.ds(8, 8), :],
                    dst_ref=buf.at[:, :, pl.ds(to, 8), :],
                    send_sem=z_sem.at[which, 0, i],
                    recv_sem=z_sem.at[which, 1, i],
                    device_id=peer,
                    device_id_type=MESH,
                ),
            )
            for i, (to, peer, out, back) in enumerate(((0, zup, has_up, has_dn), (16, zdn, has_dn, has_up)))
        ]

    g_copies = zcopies(G, 0)
    start_if(g_copies)

    wait_recv_if(p_copies)
    for f in range(2):
        for r in range(2):
            v = sums[2 * f + r] + cv * QP[f, r] + cv * QN[f, r]
            for t, v in enumerate(tiles_of(ring_extended(v))):
                fs[pl.ds(t * 4 + f * 2 + r, 8, stride=QF), :] = v
    f_copies = a2a(fs, fr, QF, 1)
    for c in f_copies:
        c.start()
    own(fs, fr, QF)

    def finish_level(k, _):
        pl.when(has_next)(bulk(k, 0).wait_recv)
        pl.when(has_prev)(bulk(k, 1).wait_recv)
        for f in range(2):
            p0, p1 = RP[k, f, 0], RP[k, f, 1]
            n0, n1 = RN[k, f, 0], RN[k, f, 1]
            for r in range(2):
                if r == 0:
                    add = cv * (16.0 * p1 - p0) - cv * n0
                else:
                    add = cv * (16.0 * n0 - n1) - cv * p1
                ST[k, f, r] = ST[k, f, r] + add
        return 0

    for c in f_copies:
        c.wait_recv()
    for f in range(2):
        for r in range(2):
            for t in range(TT + 1):
                B[f, r, 8:16, t * T : (t + 1) * T] = fr[pl.ds(t * 4 + f * 2 + r, 8, stride=QF), :]
    b_copies = zcopies(B, 1)
    start_if(b_copies)
    start_bulk(B2, B3)
    lax.fori_loop(0, F2, finish_level, 0)
    wait_recv_if(g_copies)
    wait_recv_if(b_copies)

    row = lax.broadcasted_iota(jnp.int32, (24, T), 0)
    inside = jnp.logical_and(jnp.logical_or(row >= 8, has_dn), jnp.logical_or(row < 16, has_up))
    step = jnp.concatenate([jnp.where(inside, continuity / 12.0, 0.0)] * (TT + 1), axis=1)
    east = [B[0, r] for r in range(2)]
    north = [B[1, r] for r in range(2)]
    high = [G[0, r] for r in range(2)]
    deep = [G[1, r] * (pressure / 12.0) for r in range(2)]
    for _ in range(NSUB):
        dn = dy12(north[0], north[1])
        high = [high[r] - step * (dx12(east[r]) + dn[r]) for r in range(2)]
        dh = dy12(high[0], high[1])
        east = [east[r] - deep[r] * dx12(high[r]) for r in range(2)]
        north = [north[r] - deep[r] * dh[r] for r in range(2)]
    for f, field in ((0, east), (1, north)):
        for r in range(2):
            change = field[r][8:16, :W] - B[f, r, 8:16, :W]
            for t, v in enumerate(tiles_of(change)):
                cs[pl.ds(t * 4 + f * 2 + r, 8, stride=QC), :] = v
    c_copies = a2a(cs, cr, QC, 2)
    for c in c_copies:
        c.start()
    start_bulk(B3, K)
    for r in range(2):
        for t in range(TT):
            so[pl.ds(t * 16 + r, 8, stride=2), :] = high[r][8:16, t * T : (t + 1) * T]
    own(cs, cr, QC)
    lax.fori_loop(F2, K, finish_level, 0)
    for c in c_copies:
        c.wait_recv()
    for f in range(2):
        for r in range(2):
            v = jnp.concatenate(
                [cr[pl.ds(t * 4 + f * 2 + r, 8, stride=QC), :] for t in range(TT)], axis=1
            )
            X[f, r] = v * inv[r]

    def store_level(k, _):
        for r in range(2):
            wet = lev[r] > k
            for f, dst in ((0, eo), (1, no)):
                v = jnp.where(wet, ST[k, f, r] + X[f, r], 0.0)
                for t in range(TT):
                    dst[pl.ds(k * PK + t * 2 + r, 8, stride=2 * TT), :] = v[:, t * T : (t + 1) * T]
        return 0

    lax.fori_loop(0, K, store_level, 0)

    def drain(k, _):
        pl.when(has_prev)(bulk(k, 0).wait_send)
        pl.when(has_next)(bulk(k, 1).wait_send)
        return 0

    lax.fori_loop(0, K, drain, 0)
    for c in d_copies + h_copies + f_copies + c_copies:
        c.wait_send()
    for c in (l_copies, p_copies, g_copies, b_copies):
        wait_send_if(c)


def store_kernel(e, n, h, eo, no, ho, sem, h_sem):
    TT = ho.shape[1] // T
    copies = [pltpu.make_async_copy(e, eo, sem.at[0]), pltpu.make_async_copy(n, no, sem.at[1])]
    copies += [
        pltpu.make_async_copy(h.at[pl.ds(t * 16, 16), :], ho.at[:, pl.ds(t * T, T)], h_sem.at[t])
        for t in range(TT)
    ]
    for c in copies:
        c.start()
    for c in copies:
        c.wait()


def flattened(x):
    k = x.shape[1]
    x = x.reshape(2, k, -1, T).transpose(1, 2, 0, 3)
    return x.reshape(-1, T)


def unflattened(x, k):
    x = x.reshape(k, -1, 2, T).transpose(2, 0, 1, 3)
    return x.reshape(2, k, -1)


def body(NB, NS, east_flow, north_flow, levels, coriolis, thickness, surface):
    _, K, NL = east_flow.shape
    W = NL // NS
    TT = W // T
    L = W + T
    rows = K * 2 * NL // T
    QF, QD, QC = up8((TT + 1) * 4), up8((TT + 1) * 2), up8(TT * 4)
    f32 = jnp.float32
    lev = levels.reshape(2, -1, T).transpose(1, 0, 2).reshape(-1, T)
    any_ = pl.BlockSpec(memory_space=pl.ANY)
    hbm = pl.BlockSpec(memory_space=pltpu.HBM)
    vmem = pl.BlockSpec(memory_space=pltpu.VMEM)
    big = pltpu.VMEM((K, 2, 2, 8, W), f32)
    sums = pltpu.VMEM((2, 2, 8, W), f32)
    dma = pltpu.SemaphoreType.DMA
    eo, no, so = pl.pallas_call(
        functools.partial(kernel, NB, NS, K, NL),
        out_shape=(
            jax.ShapeDtypeStruct((rows, T), f32),
            jax.ShapeDtypeStruct((rows, T), f32),
            jax.ShapeDtypeStruct((16 * TT, T), f32),
        ),
        in_specs=[hbm] * 6,
        out_specs=[vmem] * 3,
        scratch_shapes=[
            pltpu.SMEM((K,), f32),
            pltpu.SMEM((2,), f32),
            pltpu.VMEM((rows, T), f32),
            pltpu.VMEM((rows, T), f32),
            pltpu.VMEM((2 * NL // T, T), jnp.int32),
            pltpu.VMEM((16 * TT, T), f32),
            pltpu.VMEM((2, 8, W), jnp.int32),
            big,
            big,
            big,
            big,
            pltpu.VMEM((NS * QF, T), f32),
            pltpu.VMEM((NS * QF, T), f32),
            pltpu.VMEM((NS * QD, T), f32),
            pltpu.VMEM((NS * QD, T), f32),
            pltpu.VMEM((2, 2, 24, L), f32),
            pltpu.VMEM((2, 2, 24, L), f32),
            pltpu.VMEM((2, 2, 8, T), f32),
            pltpu.VMEM((NS * QC, T), f32),
            pltpu.VMEM((NS * QC, T), f32),
            sums,
            pltpu.VMEM((2, 8, W), f32),
            pltpu.VMEM((2 * NL // T, T), jnp.int32),
            pltpu.VMEM((2 * NL // T, T), jnp.int32),
            pltpu.VMEM((2, 2, 8, W), jnp.int32),
            sums,
            sums,
            sums,
            sums,
            dma((5,)),
            dma((TT,)),
            dma((2, 2, K)),
            dma((3, 2, NS - 1)),
            dma((2, 2, 2)),
            dma((2, 2)),
            dma((2, 2, 2)),
        ],
        compiler_params=pltpu.CompilerParams(
            collective_id=0, has_side_effects=True, vmem_limit_bytes=VMEM_LIMIT
        ),
    )(*[pltpu.with_memory_space_constraint(x, pltpu.HBM) for x in (thickness, coriolis, flattened(east_flow), flattened(north_flow), lev, surface)])
    eo, no, so = pl.pallas_call(
        store_kernel,
        out_shape=(
            jax.ShapeDtypeStruct((rows, T), f32),
            jax.ShapeDtypeStruct((rows, T), f32),
            jax.ShapeDtypeStruct((16, W), f32),
        ),
        in_specs=[any_] * 3,
        out_specs=[hbm] * 3,
        scratch_shapes=[dma((2,)), dma((TT,))],
        compiler_params=pltpu.CompilerParams(vmem_limit_bytes=VMEM_LIMIT),
    )(eo, no, so)
    return unflattened(eo, K), unflattened(no, K), so


def solution(mesh):
    NB, NS = mesh.shape["blk"], mesh.shape["sub"]
    both = ("blk", "sub")
    return jax.shard_map(
        functools.partial(body, NB, NS),
        mesh=mesh,
        in_specs=(P(both, None, None), P(both, None, None), P(both, None), P(both), P(), P("blk", "sub")),
        out_specs=(P(both, None, None), P(both, None, None), P("blk", "sub")),
        check_vma=False,
    )
```

time: 68.3 us -> 55.3 us (0.81)
  the two profiles are of different devices: /device:TPU:1 before, /device:TPU:32 now
where the time goes in v2:
time: 55.3 us; the launch traced here: 55.1 us
  Pallas kernels  54.4 us (98%)
  between operations  0.64 us (1%)
    pallas_call x1, Pallas kernels, body(): pl.pallas_call(functools.partial(kernel, NB, NS, K, NL), out_shape=(jax.S...  53.2 us
    pallas_call x1, Pallas kernels, body(): pl.pallas_call(store_kernel, out_shape=(jax.ShapeDtypeStruct((rows, T), f...  1.19 us

profile of v2, /device:TPU:32, one launch (start us, length us, event | category | flops | bytes accessed | tf_op | source)
XLA Modules:
  0.0 55.1 jit_solution(17606393925711456180)
XLA Ops:
  0.6 53.2 %shard_map.85 = (f32[1344,128]{1,0:T(8,128)S(1)}, f32[1344,128]{1,0:T(8,128)S(1)}, f32[112,128]{1,0:T(8,128)S(1)}) custom-call(f32[12]{0:T(128)} %t_hbm.1, f32[2]{0:T(128)} %c_hbm.1, f32[1344,128]{1,0:T(8,128)} %bitcast.25, f32[1344,128]{1,0:T(8,128)} %bitcast.26, s32[112,128]{1,0:T(8,128)} %bitcast.27, f32[16,896]{1,0:T(8,128)} %h_hbm.1), custom_call_target="tpu_custom_call" | custom-call | tf_op jit(solution)/shard_map/pallas_call | solution.py:485
  53.9 1.2 %shard_map.86 = (f32[1344,128]{1,0:T(8,128)}, f32[1344,128]{1,0:T(8,128)}, f32[16,896]{1,0:T(8,128)}) custom-call(f32[1344,128]{1,0:T(8,128)S(1)} %get-tuple-element.9.e, f32[1344,128]{1,0:T(8,128)S(1)} %get-tuple-element.10.n, f32[112,128]{1,0:T(8,128)S(1)} %get-tuple-element.11.h), custom_call_target="tpu_custom_call" | custom-call | tf_op jit(solution)/shard_map/pallas_call | solution.py:536

commit v3 on v2

--- a/solution.py
+++ b/solution.py
@@ -11,8 +11,10 @@
 T = 128
 NSUB = 4
 VMEM_LIMIT = 16 << 20
-B1, B2, B3 = 3, 6, 10
-F2 = 4
+INNER = (0, 3, 6, 8, 11, 11, 12)
+OUTER = (0, 3, 6, 8, 11, 11, 12)
+GROUPS = ((0, 4), (4, 12))
+F2 = 3
 FAR_FIRST = (4, 3, 5, 2, 6, 1, 7)
 viscosity = 0.05
 mixing = 0.1
@@ -61,7 +63,7 @@
     NB, NS, K, NL,
     t_hbm, c_hbm, e_hbm, n_hbm, l_hbm, h_hbm,
     eo, no, so,
-    thick, cor, ein, nin, lin, hin, lev, M, RP, RN, ST, fs, fr, ds_, dr, B, G, HX, cs, cr, X, inv,
+    thick, cor, e_in, n_in, lin, hin, lev, M, RP, RN, ST, fs, fr, ds_, dr, FB, EO, EI, G, HX, cs, cr, X, inv,
     LP, LN, levx, PP, PN, QP, QN,
     in_sem, h_sem, bulk_sem, a2a_sem, z_sem, x_sem, n_sem,
 ):
@@ -85,12 +87,30 @@
     has_dn, has_up = b > 0, b < NB - 1
     one = lambda there: jnp.where(there, 1, 0)
 
+    barrier = pltpu.get_barrier_semaphore()
+    for there, peer in ((has_prev, prev), (has_next, nxt), (has_dn, zdn), (has_up, zup)):
+
+        @pl.when(there)
+        def _():
+            pl.semaphore_signal(barrier, inc=1, device_id=peer, device_id_type=MESH)
+
+    for peer in peers:
+        pl.semaphore_signal(barrier, inc=1, device_id=peer, device_id_type=MESH)
+
     loads = [
         pltpu.make_async_copy(l_hbm, lin, in_sem.at[0]),
-        pltpu.make_async_copy(e_hbm, ein, in_sem.at[1]),
-        pltpu.make_async_copy(n_hbm, nin, in_sem.at[2]),
-        pltpu.make_async_copy(t_hbm, thick, in_sem.at[3]),
-        pltpu.make_async_copy(c_hbm, cor, in_sem.at[4]),
+        pltpu.make_async_copy(t_hbm, thick, in_sem.at[1]),
+        pltpu.make_async_copy(c_hbm, cor, in_sem.at[2]),
+    ]
+    flow_loads = [
+        pltpu.make_async_copy(
+            hbm.at[pl.ds(k * PK, (m - k) * PK), :], vmem, sem
+        )
+        for i, (k, m) in enumerate(GROUPS)
+        for hbm, vmem, sem in (
+            (e_hbm, e_in[i], in_sem.at[3 + i]),
+            (n_hbm, n_in[i], in_sem.at[3 + len(GROUPS) + i]),
+        )
     ]
     h_loads = [
         pltpu.make_async_copy(
@@ -98,18 +118,8 @@
         )
         for t in range(TT)
     ]
-    for c in loads + h_loads:
+    for c in loads + flow_loads + h_loads:
         c.start()
-    barrier = pltpu.get_barrier_semaphore()
-    for peer in peers:
-        pl.semaphore_signal(barrier, inc=1, device_id=peer, device_id_type=MESH)
-    for there, peer in ((has_prev, prev), (has_next, nxt), (has_dn, zdn), (has_up, zup)):
-
-        @pl.when(there)
-        def _():
-            pl.semaphore_signal(barrier, inc=1, device_id=peer, device_id_type=MESH)
-
-
     def clear(there, refs):
         @pl.when(jnp.logical_not(there))
         def _():
@@ -118,8 +128,10 @@
 
     clear(has_prev, [QP, LP])
     clear(has_next, [QN, LN])
-    clear(has_dn, [ref.at[i, j, pl.ds(0, 8)] for ref in (B, G) for i in range(2) for j in range(2)])
-    clear(has_up, [ref.at[i, j, pl.ds(16, 8)] for ref in (B, G) for i in range(2) for j in range(2)])
+    clear(has_dn, [G.at[i, j, pl.ds(0, 8)] for i in range(2) for j in range(2)])
+    clear(has_up, [G.at[i, j, pl.ds(16, 8)] for i in range(2) for j in range(2)])
+    clear(has_dn, [FB.at[j, pl.ds(0, 8)] for j in range(2)] + [EI.at[0]])
+    clear(has_up, [FB.at[j, pl.ds(16, 8)] for j in range(2)] + [EI.at[1]])
     for there, buf in ((has_prev, RP), (has_next, RN)):
 
         @pl.when(jnp.logical_not(there))
@@ -191,9 +203,8 @@
         at = pl.ds(pl.multiple_of(s * q, 8), q)
         dst[at, :] = src[at, :]
 
-    loads[0].wait()
-    loads[3].wait()
-    loads[4].wait()
+    for c in loads:
+        c.wait()
     levs = []
     for r in range(2):
         v = jnp.concatenate([lin[pl.ds(t * 2 + r, 8, stride=2 * TT), :] for t in range(TT)], axis=1)
@@ -229,20 +240,6 @@
     ]
     for c in h_copies:
         c.start()
-    loads[1].wait()
-    loads[2].wait()
-
-    def mask_level(k, _):
-        for r in range(2):
-            wet = lev[r] > k
-            for f, src in ((0, ein), (1, nin)):
-                v = jnp.concatenate(
-                    [src[pl.ds(k * PK + t * 2 + r, 8, stride=2 * TT), :] for t in range(TT)], axis=1
-                )
-                M[k, f, r] = jnp.where(wet, v, 0.0)
-        return 0
-
-    lax.fori_loop(0, K, mask_level, 0)
 
     def bulk(k, way):
         return pltpu.make_async_remote_copy(
@@ -254,12 +251,39 @@
             device_id_type=MESH,
         )
 
-    def start_bulk(first, last):
-        for k in range(first, last):
-            pl.when(has_prev)(bulk(k, 0).start)
-            pl.when(has_next)(bulk(k, 1).start)
-
-    start_bulk(0, B1)
+    def start_bulk(stage):
+        def some(there, way, plan):
+            @pl.when(there)
+            def _():
+                for k in range(plan[stage], plan[stage + 1]):
+                    bulk(k, way).start()
+
+        some(s > 0, 0, INNER)
+        some(jnp.logical_and(s == 0, has_prev), 0, OUTER)
+        some(s < NS - 1, 1, INNER)
+        some(jnp.logical_and(s == NS - 1, has_next), 1, OUTER)
+
+    def mask_level(first, sources):
+        def level(k, _):
+            for r in range(2):
+                wet = lev[r] > k
+                for f, src in enumerate(sources):
+                    at = (k - first) * PK + r
+                    v = jnp.concatenate(
+                        [src[pl.ds(at + t * 2, 8, stride=2 * TT), :] for t in range(TT)], axis=1
+                    )
+                    M[k, f, r] = jnp.where(wet, v, 0.0)
+            return 0
+
+        return level
+
+    for i, (k, m) in enumerate(GROUPS):
+        flow_loads[2 * i].wait()
+        flow_loads[2 * i + 1].wait()
+        lax.fori_loop(k, m, mask_level(k, (e_in[i], n_in[i])), 0)
+        if i == 0:
+            start_bulk(0)
+
     own(ds_, dr, QD)
 
     cv = viscosity / 12.0
@@ -316,7 +340,7 @@
                 dst[f, r] = part[2 * f + r]
     p_copies = to_neighbours(PN, PP, QP, QN, 1)
     start_if(p_copies)
-    start_bulk(B1, B2)
+    start_bulk(1)
     sums = lax.fori_loop(K // 2, K, local_level, sums)
 
     for c in d_copies + h_copies:
@@ -326,14 +350,14 @@
         for t in range(TT + 1):
             G[1, r, 8:16, t * T : (t + 1) * T] = dr[pl.ds(t * 2 + r, 8, stride=QD), :]
 
-    def zcopies(buf, which):
+    def zcopies(which, of):
         return [
             (
                 out,
                 back,
                 pltpu.make_async_remote_copy(
-                    src_ref=buf.at[:, :, pl.ds(8, 8), :],
-                    dst_ref=buf.at[:, :, pl.ds(to, 8), :],
+                    src_ref=of(i, 8)[0],
+                    dst_ref=of(i, to)[1],
                     send_sem=z_sem.at[which, 0, i],
                     recv_sem=z_sem.at[which, 1, i],
                     device_id=peer,
@@ -343,7 +367,7 @@
             for i, (to, peer, out, back) in enumerate(((0, zup, has_up, has_dn), (16, zdn, has_dn, has_up)))
         ]
 
-    g_copies = zcopies(G, 0)
+    g_copies = zcopies(0, lambda i, to: [G.at[:, :, pl.ds(to, 8), :]] * 2)
     start_if(g_copies)
 
     wait_recv_if(p_copies)
@@ -355,6 +379,7 @@
     f_copies = a2a(fs, fr, QF, 1)
     for c in f_copies:
         c.start()
+    start_bulk(2)
     own(fs, fr, QF)
 
     def finish_level(k, _):
@@ -373,39 +398,76 @@
 
     for c in f_copies:
         c.wait_recv()
-    for f in range(2):
-        for r in range(2):
-            for t in range(TT + 1):
-                B[f, r, 8:16, t * T : (t + 1) * T] = fr[pl.ds(t * 4 + f * 2 + r, 8, stride=QF), :]
-    b_copies = zcopies(B, 1)
+    east, north = [
+        [
+            jnp.concatenate([fr[pl.ds(t * 4 + f * 2 + r, 8, stride=QF), :] for t in range(TT + 1)], axis=1)
+            for r in range(2)
+        ]
+        for f in range(2)
+    ]
+    for r in range(2):
+        for t, v in enumerate(tiles_of(north[r])):
+            EO[0, r * (TT + 1) + t : r * (TT + 1) + t + 1, :] = v[7:8]
+            EO[1, r * (TT + 1) + t : r * (TT + 1) + t + 1, :] = v[0:1]
+    none = jnp.zeros((8, L), jnp.float32)
+    across = dy12(*[jnp.concatenate([none, v, none], axis=0) for v in north])
+    for r in range(2):
+        FB[r, 8:16, :] = dx12(east[r]) + across[r][8:16]
+    b_copies = zcopies(1, lambda i, to: [FB.at[:, pl.ds(to, 8), :]] * 2)
+    b_copies += zcopies(2, lambda i, to: [EO.at[i], EI.at[i]])
     start_if(b_copies)
-    start_bulk(B2, B3)
+    start_bulk(3)
     lax.fori_loop(0, F2, finish_level, 0)
     wait_recv_if(g_copies)
     wait_recv_if(b_copies)
+    start_bulk(4)
 
     row = lax.broadcasted_iota(jnp.int32, (24, T), 0)
     inside = jnp.logical_and(jnp.logical_or(row >= 8, has_dn), jnp.logical_or(row < 16, has_up))
     step = jnp.concatenate([jnp.where(inside, continuity / 12.0, 0.0)] * (TT + 1), axis=1)
-    east = [B[0, r] for r in range(2)]
-    north = [B[1, r] for r in range(2)]
     high = [G[0, r] for r in range(2)]
     deep = [G[1, r] * (pressure / 12.0) for r in range(2)]
-    for _ in range(NSUB):
+    edge = [
+        jnp.concatenate(
+            [
+                jnp.where(
+                    row == 7,
+                    EI[0, r * (TT + 1) + t : r * (TT + 1) + t + 1, :],
+                    jnp.where(row == 16, EI[1, r * (TT + 1) + t : r * (TT + 1) + t + 1, :], 0.0),
+                )
+                for t in range(TT + 1)
+            ],
+            axis=1,
+        )
+        for r in range(2)
+    ]
+    edge = dy12(edge[0], edge[1])
+    flow = [
+        step
+        * (
+            FB[r]
+            + jnp.concatenate([across[r][:8], edge[r][8:16], across[r][16:]], axis=0)
+        )
+        for r in range(2)
+    ]
+    high = [high[r] - flow[r] for r in range(2)]
+    dh = dy12(high[0], high[1])
+    east = [-deep[r] * dx12(high[r]) for r in range(2)]
+    north = [-deep[r] * dh[r] for r in range(2)]
+    for _ in range(NSUB - 1):
         dn = dy12(north[0], north[1])
-        high = [high[r] - step * (dx12(east[r]) + dn[r]) for r in range(2)]
+        high = [high[r] - flow[r] - step * (dx12(east[r]) + dn[r]) for r in range(2)]
         dh = dy12(high[0], high[1])
         east = [east[r] - deep[r] * dx12(high[r]) for r in range(2)]
         north = [north[r] - deep[r] * dh[r] for r in range(2)]
     for f, field in ((0, east), (1, north)):
         for r in range(2):
-            change = field[r][8:16, :W] - B[f, r, 8:16, :W]
-            for t, v in enumerate(tiles_of(change)):
+            for t, v in enumerate(tiles_of(field[r][8:16, :W])):
                 cs[pl.ds(t * 4 + f * 2 + r, 8, stride=QC), :] = v
     c_copies = a2a(cs, cr, QC, 2)
     for c in c_copies:
         c.start()
-    start_bulk(B3, K)
+    start_bulk(5)
     for r in range(2):
         for t in range(TT):
             so[pl.ds(t * 16 + r, 8, stride=2), :] = high[r][8:16, t * T : (t + 1) * T]
@@ -494,8 +556,8 @@
         scratch_shapes=[
             pltpu.SMEM((K,), f32),
             pltpu.SMEM((2,), f32),
-            pltpu.VMEM((rows, T), f32),
-            pltpu.VMEM((rows, T), f32),
+            [pltpu.VMEM(((m - k) * rows // K, T), f32) for k, m in GROUPS],
+            [pltpu.VMEM(((m - k) * rows // K, T), f32) for k, m in GROUPS],
             pltpu.VMEM((2 * NL // T, T), jnp.int32),
             pltpu.VMEM((16 * TT, T), f32),
             pltpu.VMEM((2, 8, W), jnp.int32),
@@ -507,7 +569,9 @@
             pltpu.VMEM((NS * QF, T), f32),
             pltpu.VMEM((NS * QD, T), f32),
             pltpu.VMEM((NS * QD, T), f32),
-            pltpu.VMEM((2, 2, 24, L), f32),
+            pltpu.VMEM((2, 24, L), f32),
+            pltpu.VMEM((2, up8(2 * (TT + 1)), T), f32),
+            pltpu.VMEM((2, up8(2 * (TT + 1)), T), f32),
             pltpu.VMEM((2, 2, 24, L), f32),
             pltpu.VMEM((2, 2, 8, T), f32),
             pltpu.VMEM((NS * QC, T), f32),
@@ -521,11 +585,11 @@
             sums,
             sums,
             sums,
-            dma((5,)),
+            dma((3 + 2 * len(GROUPS),)),
             dma((TT,)),
             dma((2, 2, K)),
             dma((3, 2, NS - 1)),
-            dma((2, 2, 2)),
+            dma((3, 2, 2)),
             dma((2, 2)),
             dma((2, 2, 2)),
         ],

time: 55.3 us -> 51.6 us (0.933)
  Pallas kernels: 54.4 us -> 50.8 us
    pallas_call x1, Pallas kernels: 53.2 us -> 49.6 us  [body(): pl.pallas_call(functools.partial(kernel, NB, NS, K, NL), out_shape=(jax.S...]
where the time goes in v3:
time: 51.6 us; the launch traced here: 51.4 us
  Pallas kernels  50.8 us (98%)
  between operations  0.64 us (1%)
    pallas_call x1, Pallas kernels, body(): pl.pallas_call(functools.partial(kernel, NB, NS, K, NL), out_shape=(jax.S...  49.6 us
    pallas_call x1, Pallas kernels, body(): pl.pallas_call(store_kernel, out_shape=(jax.ShapeDtypeStruct((rows, T), f...  1.19 us

profile of v3, /device:TPU:32, one launch (start us, length us, event | category | flops | bytes accessed | tf_op | source)
XLA Modules:
  0.0 51.4 jit_solution(18401929712400352339)
XLA Ops:
  0.6 49.6 %shard_map.85 = (f32[1344,128]{1,0:T(8,128)S(1)}, f32[1344,128]{1,0:T(8,128)S(1)}, f32[112,128]{1,0:T(8,128)S(1)}) custom-call(f32[12]{0:T(128)} %t_hbm.1, f32[2]{0:T(128)} %c_hbm.1, f32[1344,128]{1,0:T(8,128)} %bitcast.25, f32[1344,128]{1,0:T(8,128)} %bitcast.26, s32[112,128]{1,0:T(8,128)} %bitcast.27, f32[16,896]{1,0:T(8,128)} %h_hbm.1), custom_call_target="tpu_custom_call" | custom-call | tf_op jit(solution)/shard_map/pallas_call | solution.py:547
  50.3 1.2 %shard_map.86 = (f32[1344,128]{1,0:T(8,128)}, f32[1344,128]{1,0:T(8,128)}, f32[16,896]{1,0:T(8,128)}) custom-call(f32[1344,128]{1,0:T(8,128)S(1)} %get-tuple-element.9.e, f32[1344,128]{1,0:T(8,128)S(1)} %get-tuple-element.10.n, f32[112,128]{1,0:T(8,128)S(1)} %get-tuple-element.11.h), custom_call_target="tpu_custom_call" | custom-call | tf_op jit(solution)/shard_map/pallas_call | solution.py:600

commit v4 on v3

--- a/solution.py
+++ b/solution.py
@@ -11,8 +11,9 @@
 T = 128
 NSUB = 4
 VMEM_LIMIT = 16 << 20
-INNER = (0, 3, 6, 8, 11, 11, 12)
-OUTER = (0, 3, 6, 8, 11, 11, 12)
+PARTS = 4
+INNER = (0, 3, 6, 9, 12, 12, 12)
+OUTER = (0, 3, 6, 9, 12, 12, 12)
 GROUPS = ((0, 4), (4, 12))
 F2 = 3
 FAR_FIRST = (4, 3, 5, 2, 6, 1, 7)
@@ -62,8 +63,8 @@
 def kernel(
     NB, NS, K, NL,
     t_hbm, c_hbm, e_hbm, n_hbm, l_hbm, h_hbm,
-    eo, no, so,
-    thick, cor, e_in, n_in, lin, hin, lev, M, RP, RN, ST, fs, fr, ds_, dr, FB, EO, EI, G, HX, cs, cr, X, inv,
+    ST, X, lev, so,
+    thick, cor, e_in, n_in, lin, hin, M, RP, RN, fs, fr, ds_, dr, FB, EO, EI, G, HX, cs, cr, inv,
     LP, LN, levx, PP, PN, QP, QN,
     in_sem, h_sem, bulk_sem, a2a_sem, z_sem, x_sem, n_sem,
 ):
@@ -310,7 +311,7 @@
         return tuple(out)
 
     zeros = tuple(jnp.zeros((8, W), jnp.float32) for _ in range(4))
-    sums = lax.fori_loop(0, K // 2, local_level, zeros)
+    sums = lax.fori_loop(0, K // 3, local_level, zeros)
 
     wait_recv_if(l_copies)
     for i, src in ((0, LP), (1, LN)):
@@ -341,7 +342,7 @@
     p_copies = to_neighbours(PN, PP, QP, QN, 1)
     start_if(p_copies)
     start_bulk(1)
-    sums = lax.fori_loop(K // 2, K, local_level, sums)
+    sums = lax.fori_loop(K // 3, K, local_level, sums)
 
     for c in d_copies + h_copies:
         c.wait_recv()
@@ -482,17 +483,6 @@
             )
             X[f, r] = v * inv[r]
 
-    def store_level(k, _):
-        for r in range(2):
-            wet = lev[r] > k
-            for f, dst in ((0, eo), (1, no)):
-                v = jnp.where(wet, ST[k, f, r] + X[f, r], 0.0)
-                for t in range(TT):
-                    dst[pl.ds(k * PK + t * 2 + r, 8, stride=2 * TT), :] = v[:, t * T : (t + 1) * T]
-        return 0
-
-    lax.fori_loop(0, K, store_level, 0)
-
     def drain(k, _):
         pl.when(has_prev)(bulk(k, 0).wait_send)
         pl.when(has_next)(bulk(k, 1).wait_send)
@@ -505,15 +495,38 @@
         wait_send_if(c)
 
 
-def store_kernel(e, n, h, eo, no, ho, sem, h_sem):
-    TT = ho.shape[1] // T
-    copies = [pltpu.make_async_copy(e, eo, sem.at[0]), pltpu.make_async_copy(n, no, sem.at[1])]
-    copies += [
+def store_kernel(ST, X, lev, h, eo_hbm, no_hbm, ho, eo, no, sem, h_sem):
+    K, W = ST.shape[0], ST.shape[-1]
+    TT = W // T
+    PK = eo_hbm.shape[0] // K
+    part = K // PARTS
+    copies = [
         pltpu.make_async_copy(h.at[pl.ds(t * 16, 16), :], ho.at[:, pl.ds(t * T, T)], h_sem.at[t])
         for t in range(TT)
     ]
     for c in copies:
         c.start()
+
+    def store_level(first, dsts):
+        def level(k, _):
+            for r in range(2):
+                wet = lev[r] > k
+                for f, dst in enumerate(dsts):
+                    v = jnp.where(wet, ST[k, f, r] + X[f, r], 0.0)
+                    at = (k - first) * PK + r
+                    for t in range(TT):
+                        dst[pl.ds(at + t * 2, 8, stride=2 * TT), :] = v[:, t * T : (t + 1) * T]
+            return 0
+
+        return level
+
+    for i in range(PARTS):
+        first = i * part
+        lax.fori_loop(first, first + part, store_level(first, (eo[i], no[i])), 0)
+        for f, (src, dst) in enumerate(((eo[i], eo_hbm), (no[i], no_hbm))):
+            c = pltpu.make_async_copy(src, dst.at[pl.ds(first * PK, part * PK), :], sem.at[f, i])
+            c.start()
+            copies.append(c)
     for c in copies:
         c.wait()
 
@@ -544,15 +557,16 @@
     big = pltpu.VMEM((K, 2, 2, 8, W), f32)
     sums = pltpu.VMEM((2, 2, 8, W), f32)
     dma = pltpu.SemaphoreType.DMA
-    eo, no, so = pl.pallas_call(
+    star, change, deep, so = pl.pallas_call(
         functools.partial(kernel, NB, NS, K, NL),
         out_shape=(
-            jax.ShapeDtypeStruct((rows, T), f32),
-            jax.ShapeDtypeStruct((rows, T), f32),
+            jax.ShapeDtypeStruct((K, 2, 2, 8, W), f32),
+            jax.ShapeDtypeStruct((2, 2, 8, W), f32),
+            jax.ShapeDtypeStruct((2, 8, W), jnp.int32),
             jax.ShapeDtypeStruct((16 * TT, T), f32),
         ),
         in_specs=[hbm] * 6,
-        out_specs=[vmem] * 3,
+        out_specs=[vmem] * 4,
         scratch_shapes=[
             pltpu.SMEM((K,), f32),
             pltpu.SMEM((2,), f32),
@@ -560,8 +574,6 @@
             [pltpu.VMEM(((m - k) * rows // K, T), f32) for k, m in GROUPS],
             pltpu.VMEM((2 * NL // T, T), jnp.int32),
             pltpu.VMEM((16 * TT, T), f32),
-            pltpu.VMEM((2, 8, W), jnp.int32),
-            big,
             big,
             big,
             big,
@@ -576,7 +588,6 @@
             pltpu.VMEM((2, 2, 8, T), f32),
             pltpu.VMEM((NS * QC, T), f32),
             pltpu.VMEM((NS * QC, T), f32),
-            sums,
             pltpu.VMEM((2, 8, W), f32),
             pltpu.VMEM((2 * NL // T, T), jnp.int32),
             pltpu.VMEM((2 * NL // T, T), jnp.int32),
@@ -604,11 +615,16 @@
             jax.ShapeDtypeStruct((rows, T), f32),
             jax.ShapeDtypeStruct((16, W), f32),
         ),
-        in_specs=[any_] * 3,
+        in_specs=[vmem] * 3 + [any_],
         out_specs=[hbm] * 3,
-        scratch_shapes=[dma((2,)), dma((TT,))],
+        scratch_shapes=[
+            [pltpu.VMEM((rows // PARTS, T), f32)] * PARTS,
+            [pltpu.VMEM((rows // PARTS, T), f32)] * PARTS,
+            dma((2, PARTS)),
+            dma((TT,)),
+        ],
         compiler_params=pltpu.CompilerParams(vmem_limit_bytes=VMEM_LIMIT),
-    )(eo, no, so)
+    )(star, change, deep, so)
     return unflattened(eo, K), unflattened(no, K), so
 
 

time: 51.6 us -> 50.5 us (0.979)
  Pallas kernels: 50.8 us -> 49.6 us
    pallas_call x1, Pallas kernels: 49.6 us -> 48.4 us  [body(): pl.pallas_call(functools.partial(kernel, NB, NS, K, NL), out_shape=(jax.S...]
where the time goes in v4:
time: 50.5 us; the launch traced here: 50.3 us
  Pallas kernels  49.6 us (98%)
  between operations  0.64 us (1%)
    pallas_call x1, Pallas kernels, body(): pl.pallas_call(functools.partial(kernel, NB, NS, K, NL), out_shape=(jax.S...  48.4 us
    pallas_call x1, Pallas kernels, body(): pl.pallas_call(store_kernel, out_shape=(jax.ShapeDtypeStruct((rows, T), f...  1.26 us

profile of v4, /device:TPU:32, one launch (start us, length us, event | category | flops | bytes accessed | tf_op | source)
XLA Modules:
  0.0 50.3 jit_solution(7498843412941736254)
XLA Ops:
  0.6 48.4 %shard_map.85 = (f32[12,2,2,8,896]{4,3,2,1,0:T(8,128)S(1)}, f32[2,2,8,896]{3,2,1,0:T(8,128)S(1)}, s32[2,8,896]{2,1,0:T(8,128)S(1)}, f32[112,128]{1,0:T(8,128)S(1)}) custom-call(f32[12]{0:T(128)} %t_hbm.1, f32[2]{0:T(128)} %c_hbm.1, f32[1344,128]{1,0:T(8,128)} %bitcast.25, f32[1344,128]{1,0:T(8,128)} %bitcast.26, s32[112,128]{1,0:T(8,128)} %bitcast.27, ...), custom_call_target="tpu_custom_call" | custom-call | tf_op jit(solution)/shard_map/pallas_call | solution.py:560
  49.0 1.3 %shard_map.86 = (f32[1344,128]{1,0:T(8,128)}, f32[1344,128]{1,0:T(8,128)}, f32[16,896]{1,0:T(8,128)}) custom-call(f32[12,2,2,8,896]{4,3,2,1,0:T(8,128)S(1)} %get-tuple-element.10.ST, f32[2,2,8,896]{3,2,1,0:T(8,128)S(1)} %get-tuple-element.11.X, s32[2,8,896]{2,1,0:T(8,128)S(1)} %get-tuple-element.12.lev, f32[112,128]{1,0:T(8,128)S(1)} %get-tuple-element.13.h), custom_call_target="tpu_custom_call" | custom-call | tf_op jit(solution)/shard_map/pallas_call | solution.py:611
